TPU v7x, 32 devices: a whole 2x2x4 slice. The times are simulated.
32 devices in a mesh: dp: 2 (over y), fsdp: 4 (over x, core), tensor: 4 (over z).
Axes of the slice: x: 2, y: 2, z: 4, core: 2. Of those that a mesh axis runs over, the one named last changes fastest.
Arguments:
- activations: bfloat16 [1024, 8192], P(('dp', 'fsdp'), 'tensor'), may hold values from -6 to 6
- cotangent: bfloat16 [1024, 8192], P(('dp', 'fsdp'), 'tensor'), may hold values from -6 to 6
- up_tiles: bfloat16 [1024, 128, 128], P(('fsdp', 'tensor')), may hold values from -0.1875 to 0.1875
- down_tiles: bfloat16 [1024, 128, 128], P(('fsdp', 'tensor')), may hold values from -0.125 to 0.125
- up_rows: int32 [256, 4], P(None, 'tensor'), may hold values from 0 to 63, as said below
- up_cols: int32 [256, 4], P(None, 'tensor'), may hold values from 0 to 31, as said below
- down_rows: int32 [256, 4], P(None, 'tensor'), may hold values from 0 to 31, as said below
- down_cols: int32 [256, 4], P(None, 'tensor'), may hold values from 0 to 63, as said below
Outputs:
- output: bfloat16 [1024, 8192], P(('dp', 'fsdp'), 'tensor')
- input_grad: bfloat16 [1024, 8192], P(('dp', 'fsdp'), 'tensor')
- up_grad: float32 [1024, 128, 128], P(('fsdp', 'tensor'))
- down_grad: float32 [1024, 128, 128], P(('fsdp', 'tensor'))
Inputs may be any that keep to these rules, and one draw needn't show every extreme that they name: `up_rows`: within a column, the up tiles of one hidden-unit block name distinct feature blocks. `up_cols`: every value occurs exactly 8 times in each column. `down_rows`: every value occurs exactly 8 times in each column. `down_cols`: within a column, the down tiles of one hidden-unit block name distinct feature blocks.
All inputs are finite; a program needn't handle non-finite values.
Results may differ from a plain program's by a relative error of at most 0.018.
Values may be sent and summed in bfloat16 or wider, within the bound.
A program may use at most 128 MiB of HBM per device.

v0:
```python
import jax
import jax.numpy as jnp
from jax import lax
from jax.sharding import PartitionSpec as P

D = 8192
FF = 16384


inv_root_two = 0.7071067811865476
inv_root_tau = 0.3989422804014327


def gelu_parts(values):
    normal_cdf = 0.5 * (1.0 + jax.scipy.special.erf(values * inv_root_two))
    density = inv_root_tau * jnp.exp(-0.5 * values * values)
    return (values * normal_cdf, normal_cdf + values * density)


def grouped_pick(acting, far_index, hidden_blocks, block_size):
    rows_here = acting.shape[0]
    picked = acting.reshape(rows_here, -1, block_size)[:, far_index]
    return picked.reshape(rows_here, hidden_blocks, -1, block_size)


def add_far(product, far_index, model_blocks):
    rows_here = product.shape[0]
    block_size = product.shape[-1]
    flat = product.reshape(rows_here, -1, block_size)
    summed = (
        jnp.zeros((rows_here, model_blocks, block_size), jnp.float32).at[:, far_index].add(flat)
    )
    return summed.reshape(rows_here, model_blocks * block_size)


def grouped_tiles(tiles, order, hidden_blocks):
    block_size = tiles.shape[1]
    return tiles[order].reshape(hidden_blocks, -1, block_size, block_size)


def body(activations, cotangent, up_tiles, down_tiles, up_rows, up_cols, down_rows, down_cols):
    block_size = up_tiles.shape[1]
    hidden_blocks = FF // (block_size * lax.axis_size("tensor"))
    model_blocks = D // block_size
    up_order = jnp.argsort(up_cols[:, 0], stable=True)
    down_order = jnp.argsort(down_rows[:, 0], stable=True)
    up_back = jnp.argsort(up_order)
    down_back = jnp.argsort(down_order)
    up_far = up_rows[:, 0][up_order]
    down_far = down_cols[:, 0][down_order]
    full_input = lax.all_gather(activations, "tensor", axis=1, tiled=True)
    input_pick = grouped_pick(full_input, up_far, hidden_blocks, block_size)
    up_whole = lax.all_gather(up_tiles, "fsdp", axis=0, tiled=True)
    up_sorted = grouped_tiles(up_whole, up_order, hidden_blocks)
    pre_act = jnp.einsum(
        "thkb,hkbc->thc", input_pick, up_sorted, preferred_element_type=jnp.float32
    )
    gelu_out, gelu_slope = gelu_parts(pre_act)
    hidden = gelu_out.astype(jnp.bfloat16)
    down_whole = lax.all_gather(down_tiles, "fsdp", axis=0, tiled=True)
    down_sorted = grouped_tiles(down_whole, down_order, hidden_blocks)
    out_product = jnp.einsum(
        "thb,hkbc->thkc", hidden, down_sorted, preferred_element_type=jnp.float32
    )
    partial_out = add_far(out_product, down_far, model_blocks)
    output = lax.psum_scatter(
        partial_out.astype(jnp.bfloat16), "tensor", scatter_dimension=1, tiled=True
    )
    full_cotangent = lax.all_gather(cotangent, "tensor", axis=1, tiled=True)
    cot_pick = grouped_pick(full_cotangent, down_far, hidden_blocks, block_size)
    hidden_grad = jnp.einsum(
        "thkc,hkbc->thb", cot_pick, down_sorted, preferred_element_type=jnp.float32
    )
    pre_grad = (hidden_grad * gelu_slope).astype(jnp.bfloat16)
    in_product = jnp.einsum(
        "thc,hkbc->thkb", pre_grad, up_sorted, preferred_element_type=jnp.float32
    )
    partial_in = add_far(in_product, up_far, model_blocks)
    input_grad = lax.psum_scatter(
        partial_in.astype(jnp.bfloat16), "tensor", scatter_dimension=1, tiled=True
    )
    up_grouped = jnp.einsum(
        "thkb,thc->hkbc", input_pick, pre_grad, preferred_element_type=jnp.float32
    )
    down_grouped = jnp.einsum(
        "thb,thkc->hkbc", hidden, cot_pick, preferred_element_type=jnp.float32
    )
    up_rounded = up_grouped.astype(jnp.bfloat16).reshape(-1, block_size, block_size)
    down_rounded = down_grouped.astype(jnp.bfloat16).reshape(-1, block_size, block_size)
    up_term = up_rounded[up_back].astype(jnp.float32)
    down_term = down_rounded[down_back].astype(jnp.float32)
    replicas = lax.axis_size("dp")
    owners = lax.axis_size("fsdp")

    def regroup(grad_term):
        per_piece = grad_term.shape[0] // (replicas * owners)
        shaped = grad_term.reshape(owners, replicas, per_piece, block_size, block_size)
        return shaped.transpose(1, 0, 2, 3, 4).reshape(-1, block_size, block_size)

    up_piece, down_piece = (
        lax.psum_scatter(
            regroup(up_term).astype(jnp.bfloat16), ("dp", "fsdp"), scatter_dimension=0, tiled=True
        ).astype(jnp.float32),
        lax.psum_scatter(
            regroup(down_term).astype(jnp.bfloat16), ("dp", "fsdp"), scatter_dimension=0, tiled=True
        ).astype(jnp.float32),
    )
    up_grad, down_grad = (
        lax.all_gather(up_piece.astype(jnp.bfloat16), "dp", axis=0, tiled=True).astype(
            up_piece.dtype
        ),
        lax.all_gather(down_piece.astype(jnp.bfloat16), "dp", axis=0, tiled=True).astype(
            down_piece.dtype
        ),
    )
    return (output, input_grad, up_grad, down_grad)


def solution(mesh):
    in_specs = (
        P(("dp", "fsdp"), "tensor"),
        P(("dp", "fsdp"), "tensor"),
        P(("fsdp", "tensor"), None, None),
        P(("fsdp", "tensor"), None, None),
        P(None, "tensor"),
        P(None, "tensor"),
        P(None, "tensor"),
        P(None, "tensor"),
    )
    out_specs = (
        P(("dp", "fsdp"), "tensor"),
        P(("dp", "fsdp"), "tensor"),
        P(("fsdp", "tensor"), None, None),
        P(("fsdp", "tensor"), None, None),
    )
    return jax.shard_map(body, mesh=mesh, in_specs=in_specs, out_specs=out_specs, check_vma=False)
```

profile of v0, /device:TPU:8, one launch (start us, length us, event | category | flops | bytes accessed | tf_op | source)
XLA Modules:
  0.0 581.6 jit_solution(14450266587126344888)
XLA Ops:
  7.2 0.0 all-gather.11.cloned.1.call-start
  7.2 2.0 copy.62
  9.3 0.0 all-gather.11.cloned.1.call-update
  9.3 0.0 all-gather.13.cloned.1.call-start
  9.4 2.0 copy.69
  11.4 0.0 all-gather.13.cloned.1.call-update
  11.4 0.0 all-gather.9.cloned.1.call-start
  11.5 0.7 all-gather.9.cloned.1.call-update
  12.2 0.0 all-gather.7.cloned.1.call-start
  12.2 0.5 all-gather.7.cloned.1.call-update
  12.7 0.0 reduce-scatter.11.cloned.1.call-start
  12.8 3.8 sort.62
  16.6 3.2 sort.65
  19.8 3.8 sort.63
  23.7 1.9 gather_fusion.3
  25.7 1.9 gather_fusion
  27.7 29.7 %all-gather.11.cloned.1.call-done = bf16[128,8192]{0,1:T(8,128)(2,1)} async-done(((bf16[128,2048]{0,1:T(8,128)(2,1)}), bf16[128,8192]{0,1:T(8,128)(2,1)}) %all-gather.11.cloned.1.call-update) | async-done | bytes 2097168 | tf_op jit(solution)/shard_map/all_gather | solution.py:51
  57.4 3.2 copy.63
  60.6 43.1 %all-gather.13.cloned.1.call-done = bf16[128,8192]{0,1:T(8,128)(2,1)} async-done(((bf16[128,2048]{0,1:T(8,128)(2,1)}), bf16[128,8192]{0,1:T(8,128)(2,1)}) %all-gather.13.cloned.1.call-update) | async-done | bytes 2097168 | tf_op jit(solution)/shard_map/all_gather | solution.py:69
  103.7 4.1 copy.70
  107.8 11.1 %gather_fusion.5 = bf16[256,128,128]{2,1,0:T(8,128)(2,1)} fusion(bf16[128,64,128]{2,0,1:T(8,128)(2,1)} %copy.70, s32[1024]{0:T(1024)S(1)} %pad_clamp_fusion.2), kind=kCustom, calls=%fused_computation.5 | custom fusion | bytes 16778240 | tf_op jit(solution)/shard_map/gather | solution.py:22
  118.9 8.6 %gather_fusion.4 = bf16[256,128,128]{2,1,0:T(8,128)(2,1)} fusion(bf16[128,64,128]{2,0,1:T(8,128)(2,1)S(1)} %copy.63, s32[1024]{0:T(1024)S(1)} %pad_clamp_fusion.3), kind=kCustom, calls=%fused_computation.4 | custom fusion | bytes 16778240 | tf_op jit(solution)/shard_map/gather | solution.py:22
  127.5 36.2 %all-gather.9.cloned.1.call-done = bf16[256,128,128]{2,1,0:T(8,128)(2,1)} async-done(((bf16[64,128,128]{2,1,0:T(8,128)(2,1)}), bf16[256,128,128]{2,1,0:T(8,128)(2,1)}) %all-gather.9.cloned.1.call-update) | async-done | bytes 8388624 | tf_op jit(solution)/shard_map/all_gather | solution.py:53
  163.7 13.1 %gather_fusion.2 = bf16[256,128,128]{2,1,0:T(8,128)(2,1)} fusion(bf16[256,128,128]{2,1,0:T(8,128)(2,1)} %all-gather.9.cloned.1.call-done, s32[1024]{0:T(1024)S(1)} %pad_clamp_fusion.4), kind=kCustom, calls=%fused_computation.2 | custom fusion | bytes 16778240 | tf_op jit(solution)/shard_map/gather | solution.py:38
  176.8 8.7 %fusion.15 = f32[32,128,128,1]{2,1,3,0:T(8,128)S(1)} fusion(bf16[32,8,128,128]{3,2,1,0:T(8,128)(2,1)} %bitcast.97, bf16[128,32,8,128]{3,0,2,1:T(8,128)(2,1)} %bitcast.99), kind=kOutput, calls=%fused_computation.40 | convolution fusion | flops 1073741824 | bytes 18874368 | tf_op jit(solution)/shard_map/thkb,hkbc->thc/dot_general | solution.py:55
  185.5 9.3 %convolution_convert_fusion = bf16[32,8,128,128]{3,2,1,0:T(8,128)(2,1)} fusion(bf16[128,32,8,128]{3,0,2,1:T(8,128)(2,1)} %bitcast.106, f32[32,128,128,1]{2,1,3,0:T(8,128)S(1)} %fusion.15), kind=kOutput, calls=%fused_computation.10 | convolution fusion | flops 1080557568 | bytes 18874368 | tf_op jit(solution)/shard_map/thb,thkc->hkbc/dot_general | solution.py:85
  194.8 12.1 %gather_fusion.7 = bf16[256,128,128]{1,2,0:T(8,128)(2,1)} fusion(bf16[256,128,128]{1,2,0:T(8,128)(2,1)} %bitcast.113, s32[1024]{0:T(1024)S(1)} %pad_clamp_fusion), kind=kCustom, calls=%fused_computation.7 | custom fusion | bytes 16778240 | tf_op jit(solution)/shard_map/gather | solution.py:91
  206.9 12.0 %copy.79 = bf16[4,2,32,128,128]{4,3,2,0,1:T(8,128)(2,1)} copy(bf16[4,2,32,128,128]{3,4,2,1,0:T(8,128)(2,1)} %bitcast.110) | data formatting | bytes 16777216 | tf_op jit(solution)/shard_map/convert_element_type | solution.py:105
  218.9 0.0 reduce-scatter.9.cloned.1.call-start
  219.0 3.2 sort.64
  222.1 1.3 all-gather.7.cloned.1.call-done
  223.4 12.5 %gather_fusion.1 = bf16[256,128,128]{2,1,0:T(8,128)(2,1)} fusion(bf16[256,128,128]{2,1,0:T(8,128)(2,1)} %all-gather.7.cloned.1.call-done, s32[1024]{0:T(1024)S(1)} %pad_clamp_fusion.5), kind=kCustom, calls=%fused_computation.1 | custom fusion | bytes 16778240 | tf_op jit(solution)/shard_map/gather | solution.py:38
  236.0 10.9 %fusion.10 = bf16[128,32,128,1]{0,2,3,1:T(8,128)(2,1)S(1)} fusion(f32[32,128,128,1]{2,1,3,0:T(8,128)S(1)} %fusion.15, bf16[32,8,128,128]{3,2,1,0:T(8,128)(2,1)} %bitcast.108, bf16[128,32,8,128]{3,0,2,1:T(8,128)(2,1)} %bitcast.107), kind=kOutput, calls=%fused_computation.25 | convolution fusion | flops 1078984704 | bytes 19922944 | tf_op jit(solution)/shard_map/thkc,hkbc->thb/dot_general | solution.py:71
  246.9 9.1 %convolution_convert_fusion.1 = bf16[32,8,128,128]{3,2,1,0:T(8,128)(2,1)} fusion(bf16[128,32,8,128]{3,0,2,1:T(8,128)(2,1)} %bitcast.100, bf16[128,32,128,1]{0,2,3,1:T(8,128)(2,1)S(1)} %fusion.10), kind=kOutput, calls=%fused_computation.11 | convolution fusion | flops 1077936128 | bytes 17825792 | tf_op jit(solution)/shard_map/thkb,thc->hkbc/dot_general | solution.py:82
  255.9 12.2 %gather_fusion.6 = bf16[256,128,128]{2,1,0:T(8,128)(2,1)} fusion(bf16[256,128,128]{2,1,0:T(8,128)(2,1)} %bitcast.111, s32[1024]{0:T(1024)S(1)} %pad_clamp_fusion.1), kind=kCustom, calls=%fused_computation.6 | custom fusion | bytes 16778240 | tf_op jit(solution)/shard_map/gather | solution.py:90
  268.2 10.4 %copy.76 = bf16[4,2,32,128,128]{4,3,2,0,1:T(8,128)(2,1)} copy(bf16[4,2,32,128,128]{4,3,2,1,0:T(8,128)(2,1)} %bitcast.112) | data formatting | bytes 16777216 | tf_op jit(solution)/shard_map/convert_element_type | solution.py:102
  278.6 0.3 reduce-scatter.5.cloned.1.call-start
  278.9 11.6 %fusion.13 = f32[32,8,128,128]{3,2,1,0:T(8,128)} fusion(bf16[32,8,128,128]{3,2,1,0:T(8,128)(2,1)} %bitcast.109, f32[32,128,128,1]{2,1,3,0:T(8,128)S(1)} %fusion.15), kind=kOutput, calls=%fused_computation.39 | convolution fusion | flops 1076363264 | bytes 27262976 | tf_op jit(solution)/shard_map/thb,hkbc->thkc/dot_general | solution.py:62
  290.5 17.5 %copy.67 = f32[128,256,128]{2,0,1:T(8,128)} copy(f32[128,256,128]{0,2,1:T(8,128)} %bitcast.103) | data formatting | bytes 33554432 | tf_op jit(solution)/shard_map/reshape | solution.py:29
  308.0 2.6 broadcast.42.clone
  310.6 52.3 %scatter_fusion = f32[128,64,128]{2,0,1:T(8,128)} fusion(f32[128,64,128]{2,0,1:T(8,128)} %broadcast.42.clone, s32[256]{0:T(256)S(1)} %bitcast.121, f32[256,128,128]{2,1,0:T(8,128)} %bitcast.102), kind=kCustom, calls=%fused_computation.8 | custom fusion | flops 4194304 | bytes 50332672 | tf_op jit(solution)/shard_map/scatter-add | solution.py:31
  362.9 2.6 convert_element_type.64
  365.4 2.9 copy.68
  368.4 0.0 reduce-scatter.7.cloned.1.call-start
  368.4 11.5 %fusion.16 = f32[32,8,128,128]{3,2,1,0:T(8,128)} fusion(bf16[32,8,128,128]{3,2,1,0:T(8,128)(2,1)} %bitcast.98, bf16[128,32,128,1]{0,2,3,1:T(8,128)(2,1)S(1)} %fusion.10), kind=kOutput, calls=%fused_computation.41 | convolution fusion | flops 1073741824 | bytes 26214400 | tf_op jit(solution)/shard_map/thc,hkbc->thkb/dot_general | solution.py:75
  379.9 17.5 %copy.72 = f32[128,256,128]{2,0,1:T(8,128)} copy(f32[128,256,128]{0,2,1:T(8,128)} %bitcast.96) | data formatting | bytes 33554432 | tf_op jit(solution)/shard_map/reshape | solution.py:29
  397.4 2.5 broadcast.42.clone.1
  400.0 51.3 %scatter_fusion.1 = f32[128,64,128]{2,0,1:T(8,128)} fusion(f32[128,64,128]{2,0,1:T(8,128)} %broadcast.42.clone.1, s32[256]{0:T(256)S(1)} %bitcast.119, f32[256,128,128]{2,1,0:T(8,128)} %bitcast.101), kind=kCustom, calls=%fused_computation.9 | custom fusion | flops 4194304 | bytes 50332672 | tf_op jit(solution)/shard_map/scatter-add | solution.py:31
  451.3 2.6 convert_element_type.67
  453.8 2.9 copy.73
  456.8 0.0 all-gather.17.cloned.1.call-start
  456.8 0.0 reduce-scatter.11.cloned.1.call-done
  456.8 0.6 all-gather.17.cloned.1.call-update
  457.5 0.0 all-gather.15.cloned.1.call-start
  457.5 0.0 reduce-scatter.9.cloned.1.call-done
  457.6 0.5 all-gather.15.cloned.1.call-update
  458.1 0.0 reduce-scatter.5.cloned.1.call-done
  458.1 2.0 copy.80
  460.1 40.8 %reduce-scatter.7.cloned.1.call-done = bf16[128,2048]{0,1:T(8,128)(2,1)} async-done(((bf16[128,8192]{0,1:T(8,128)(2,1)}), bf16[128,2048]{0,1:T(8,128)(2,1)}) %reduce-scatter.7.cloned.1.call-update) | async-done | bytes 524304 | tf_op jit(solution)/shard_map/reduce_scatter | solution.py:79
  501.0 2.0 copy.81
  503.0 32.7 %all-gather.17.cloned.1.call-done = bf16[64,128,128]{2,1,0:T(8,128)(2,1)} async-done(((bf16[32,128,128]{2,1,0:T(8,128)(2,1)}), bf16[64,128,128]{2,1,0:T(8,128)(2,1)}) %all-gather.17.cloned.1.call-update) | async-done | bytes 2097168 | tf_op jit(solution)/shard_map/all_gather | solution.py:112
  535.7 4.1 convert_element_type.79
  539.8 30.4 %all-gather.15.cloned.1.call-done = bf16[64,128,128]{2,1,0:T(8,128)(2,1)} async-done(((bf16[32,128,128]{2,1,0:T(8,128)(2,1)}), bf16[64,128,128]{2,1,0:T(8,128)(2,1)}) %all-gather.15.cloned.1.call-update) | async-done | bytes 2097168 | tf_op jit(solution)/shard_map/all_gather | solution.py:109
  570.2 4.1 convert_element_type.73
  (26 shorter events, 0.2 us)
Async XLA Ops:
  7.2 16.5 %copy-start = (s32[256,1]{0,1:T(1,128)S(1)}, s32[256,1]{0,1:T(1,128)}, u32[]{:S(2)}) copy-start(s32[256,1]{0,1:T(1,128)} %param.12) | copy-start | bytes 3076
  7.2 18.5 %copy-start.2 = (s32[256,1]{0,1:T(1,128)S(1)}, s32[256,1]{0,1:T(1,128)}, u32[]{:S(2)}) copy-start(s32[256,1]{0,1:T(1,128)} %param.15) | copy-start | bytes 3076
  7.2 50.2 %all-gather.11.cloned.1.call-start = ((), (), s32[]{:S(2)}) async-start(), calls=%async_computation.6 | async-start | bytes 2621440 | tf_op jit(solution)/shard_map/all_gather | solution.py:51
  9.3 94.4 %all-gather.13.cloned.1.call-start = ((), (), s32[]{:S(2)}) async-start(), calls=%async_computation.8 | async-start | bytes 2621440 | tf_op jit(solution)/shard_map/all_gather | solution.py:69
  11.4 152.3 %all-gather.9.cloned.1.call-start = ((), (), s32[]{:S(2)}) async-start(), calls=%async_computation.5 | async-start | bytes 10485760 | tf_op jit(solution)/shard_map/all_gather | solution.py:53
  12.2 211.3 %all-gather.7.cloned.1.call-start = ((), (), s32[]{:S(2)}) async-start(), calls=%async_computation.4 | async-start | bytes 10485760 | tf_op jit(solution)/shard_map/all_gather | solution.py:60
  12.7 444.1 %reduce-scatter.11.cloned.1.call-start = ((), (), s32[]{:S(2)}) async-start(), calls=%async_computation.12 | async-start | bytes 9437184 | tf_op jit(solution)/shard_map/reduce_scatter | solution.py:104
  218.9 238.7 %reduce-scatter.9.cloned.1.call-start = ((), (), s32[]{:S(2)}) async-start(), calls=%async_computation.10 | async-start | bytes 9437184 | tf_op jit(solution)/shard_map/reduce_scatter | solution.py:101
  278.6 179.5 %reduce-scatter.5.cloned.1.call-start = ((), (), s32[]{:S(2)}) async-start(), calls=%async_computation.7 | async-start | bytes 2621440 | tf_op jit(solution)/shard_map/reduce_scatter | solution.py:66
  368.4 132.6 %reduce-scatter.7.cloned.1.call-start = ((), (), s32[]{:S(2)}) async-start(), calls=%async_computation.9 | async-start | bytes 2621440 | tf_op jit(solution)/shard_map/reduce_scatter | solution.py:79
  456.8 78.9 %all-gather.17.cloned.1.call-start = ((), (), s32[]{:S(2)}) async-start(), calls=%async_computation.13 | async-start | bytes 3145728 | tf_op jit(solution)/shard_map/all_gather | solution.py:112
  456.8 117.5 %copy-start.1 = (s32[256,1]{0,1:T(1,128)S(1)}, s32[256,1]{0,1:T(1,128)}, u32[]{:S(2)}) copy-start(s32[256,1]{0,1:T(1,128)} %param.12) | copy-start | bytes 3076
  457.5 112.7 %all-gather.15.cloned.1.call-start = ((), (), s32[]{:S(2)}) async-start(), calls=%async_computation.11 | async-start | bytes 3145728 | tf_op jit(solution)/shard_map/all_gather | solution.py:109
Sparse Core Ops, SparseCore 0:
  10.1 47.2 all-gather.10
  59.6 44.1 all-gather.12
  105.3 58.3 all-gather.8
  165.1 58.2 all-gather.6
  226.7 71.5 reduce-scatter.10
  301.7 71.4 reduce-scatter.8
  376.1 42.7 reduce-scatter.4
  456.9 44.0 reduce-scatter.6
  502.5 33.0 all-gather.16
  537.0 33.0 all-gather.14
where the time goes:
time: 593 us; the launch traced here: 582 us
  waiting for transfers between devices  217 us (37%)
  local copies, waits for them, and re-layouts  157 us (26%)
  other arithmetic  131 us (22%)
  matrix products  61.1 us (10%)
  between operations  14.8 us (2%)
    scatter-add x2, other arithmetic, add_far(): jnp.zeros((rows_here, model_blocks, block_size), jnp.float32)  104 us
    all_gather x1, waiting for transfers between devices, body(): full_cotangent = lax.all_gather(cotangent, 'tensor', axis=1, tiled=True)  43.1 us
    reduce_scatter x1, waiting for transfers between devices, body(): lax.psum_scatter(partial_in.astype(jnp.bfloat16), 'tensor', scatter_dimen...  40.8 us
    all_gather x1, waiting for transfers between devices, body(): up_whole = lax.all_gather(up_tiles, 'fsdp', axis=0, tiled=True)  36.2 us
    reshape x2, local copies, waits for them, and re-layouts, add_far(): flat = product.reshape(rows_here, -1, block_size)  35 us
    all_gather x1, waiting for transfers between devices, body(): lax.all_gather(down_piece.astype(jnp.bfloat16), 'dp', axis=0, tiled=True)  32.7 us
    all_gather x1, waiting for transfers between devices, body(): lax.all_gather(up_piece.astype(jnp.bfloat16), 'dp', axis=0, tiled=True)  30.4 us
    all_gather x1, waiting for transfers between devices, body(): full_input = lax.all_gather(activations, 'tensor', axis=1, tiled=True)  29.7 us
  transfers between devices with their start and end apart: 10, of which 7 were waited for; matrix products, arithmetic and copies ran while one was open for 59% of the time, Pallas kernels for 0%

commit v1 on v0

v1 whole, which is shorter than its diff:
```python
import functools
from itertools import zip_longest

import jax
import jax.numpy as jnp
from jax import lax
from jax.experimental import pallas as pl
from jax.experimental.pallas import tpu as pltpu
from jax.sharding import PartitionSpec as P

MESH = pl.DeviceIdType.MESH
COL_TILES = 8
PIECES = 4

inv_root_two = 0.7071067811865476
inv_root_tau = 0.3989422804014327


def gelu_parts(values):
    normal_cdf = 0.5 * (1.0 + lax.erf(values * inv_root_two))
    density = inv_root_tau * jnp.exp(-0.5 * values * values)
    return (values * normal_cdf, normal_cdf + values * density)


def remote(src, dst, send_sem, recv_sem, where):
    return pltpu.make_async_remote_copy(
        src_ref=src, dst_ref=dst, send_sem=send_sem, recv_sem=recv_sem,
        device_id=where, device_id_type=MESH,
    )


def place(sizes):
    n, chips, replicas = sizes
    z = lax.axis_index("tensor")
    f = lax.axis_index("fsdp")
    y = lax.axis_index("dp")
    return z, f // 2, f % 2, y


def enter(sizes):
    n, chips, replicas = sizes
    z, r, c, y = place(sizes)
    barrier = pltpu.get_barrier_semaphore()

    def greet(where):
        pl.semaphore_signal(barrier, inc=1, device_id=where, device_id_type=MESH)

    @pl.when(z < n - 1)
    def _():
        greet({"tensor": z + 1})

    @pl.when(z > 0)
    def _():
        greet({"tensor": z - 1})

    greet({"fsdp": r * 2 + 1 - c})
    for d in range(1, chips):
        greet({"fsdp": lax.rem(r + d, chips) * 2 + c})
    for e in range(1, replicas):
        greet({"dp": lax.rem(y + e, replicas)})
    sides = jnp.where(z < n - 1, 1, 0) + jnp.where(z > 0, 1, 0)
    pl.semaphore_wait(barrier, sides + 1 + (chips - 1) + (replicas - 1))


def gather_kernel(
    sizes, act, cot, up, down, x_all, c_all, u_all, d_all,
    own_x, own_c, own_u, own_d,
    load_sem, keep_sem, zs_sem, zr_sem, xs_sem, xr_sem, ys_sem, yr_sem, cs_sem, cr_sem,
):
    n, chips, replicas = sizes
    z, r, c, y = place(sizes)
    f = r * 2 + c
    blocks = own_x.shape[0]
    per = up.shape[0]
    part = per // replicas
    features = ((act, own_x, x_all), (cot, own_c, c_all))
    weights = ((up, own_u, u_all), (down, own_d, d_all))

    loads = []
    for a, (src, own, _) in enumerate(features):
        for b in range(blocks):
            copy = pltpu.make_async_copy(
                src.at[:, pl.ds(b * 128, 128)], own.at[b], load_sem.at[a, b]
            )
            copy.start()
            loads.append(copy)
    for a, (src, own, _) in enumerate(weights):
        copy = pltpu.make_async_copy(src, own, load_sem.at[2 + a, 0])
        copy.start()
    enter(sizes)
    for copy in loads:
        copy.wait()

    def shard(full, s):
        return full.at[pl.ds(s * blocks, blocks)]

    def line(a, s, way, source):
        _, own, full = features[a]
        k = 0 if way > 0 else 1
        mine = own if source else shard(full, z - way * s)
        return remote(
            mine, shard(full, z - way * s), zs_sem.at[a, k, s], zr_sem.at[a, k, s],
            {"tensor": z + way},
        )

    def can_send(way):
        return z < n - 1 if way > 0 else z > 0

    def has(s, way):
        return z - s >= 0 if way > 0 else z + s <= n - 1

    for a in range(2):
        for way in (1, -1):

            @pl.when(can_send(way))
            def _():
                line(a, 0, way, True).start()

    def tile_range(full, r_of, c_of, q):
        return full.at[pl.ds((r_of * 2 + c_of) * per + q * part, part)]

    def x_copy(a, d):
        src = weights[a][0].at[pl.ds(y * part, part)]
        return remote(
            src, tile_range(weights[a][2], r, c, y), xs_sem.at[a, d], xr_sem.at[a, d],
            {"fsdp": lax.rem(r + d, chips) * 2 + c},
        )

    for a in range(2):
        for d in range(1, chips):
            x_copy(a, d).start()

    def own_core(a):
        full = weights[a][2]
        return remote(
            weights[a][0], full.at[pl.ds(f * per, per)], cs_sem.at[a, 0, 0], cr_sem.at[a, 0, 0],
            {"fsdp": r * 2 + 1 - c},
        )

    for a in range(2):
        own_core(a).start()

    keeps = []
    for a, (_, own, full) in enumerate(features):
        keeps.append(pltpu.make_async_copy(own, shard(full, z), keep_sem.at[a]))
    for a, (src, own, full) in enumerate(weights):
        pltpu.make_async_copy(src, own, load_sem.at[2 + a, 0]).wait()
        keeps.append(
            pltpu.make_async_copy(own, full.at[pl.ds(f * per, per)], keep_sem.at[2 + a])
        )
    for copy in keeps:
        copy.start()

    def y_copy(a, d, e):
        piece = tile_range(weights[a][2], lax.rem(r - d + chips, chips), c, y)
        return remote(
            piece, piece, ys_sem.at[a, d, e], yr_sem.at[a, d, e],
            {"dp": lax.rem(y + e, replicas)},
        )

    def core_copy(a, d, e):
        q = lax.rem(y - e + replicas, replicas)
        piece = tile_range(weights[a][2], lax.rem(r - d + chips, chips), c, q)
        return remote(
            piece, piece, cs_sem.at[a, d, e], cr_sem.at[a, d, e], {"fsdp": r * 2 + 1 - c}
        )

    def z_event(s):
        for a in range(2):
            for way in (1, -1):

                @pl.when(has(s, way))
                def _():
                    line(a, s - 1, way, False).wait_recv()

                    if s < n - 1:

                        @pl.when(can_send(way))
                        def _():
                            line(a, s, way, False).start()

    def x_event(a):
        for d in range(1, chips):
            x_copy(a, d).wait_recv()
            for e in range(1, replicas):
                y_copy(a, d, e).start()
            core_copy(a, d, 0).start()

    def y_event(a):
        for d in range(1, chips):
            for e in range(1, replicas):
                y_copy(a, d, e).wait_recv()
                core_copy(a, d, e).start()

    tile_events = [
        lambda: x_event(0),
        lambda: (x_event(1), y_event(0)),
        lambda: y_event(1),
    ]
    z_events = [functools.partial(z_event, s) for s in range(1, n)]
    for first, second in zip_longest(z_events, tile_events):
        if first is not None:
            first()
        if second is not None:
            second()

    for copy in keeps:
        copy.wait()
    for a in range(2):
        own_core(a).wait()
        for d in range(1, chips):
            x_copy(a, d).wait_send()
            core_copy(a, d, 0).wait()
            for e in range(1, replicas):
                y_copy(a, d, e).wait_send()
                core_copy(a, d, e).wait()
        for way in (1, -1):
            for s in range(n - 1):

                @pl.when(jnp.logical_and(can_send(way), has(s, way)))
                def _():
                    line(a, s, way, s == 0).wait_send()


def gather(sizes, activations, cotangent, up_tiles, down_tiles):
    n, chips, replicas = sizes
    rows, wide = activations.shape
    blocks = wide // 128
    per = up_tiles.shape[0]
    kind = jnp.bfloat16
    dma = pltpu.SemaphoreType.DMA
    anywhere = pl.BlockSpec(memory_space=pl.ANY)
    return pl.pallas_call(
        functools.partial(gather_kernel, sizes),
        out_shape=(
            jax.ShapeDtypeStruct((n * blocks, rows, 128), kind),
            jax.ShapeDtypeStruct((n * blocks, rows, 128), kind),
            jax.ShapeDtypeStruct((2 * chips * per, 128, 128), kind),
            jax.ShapeDtypeStruct((2 * chips * per, 128, 128), kind),
        ),
        in_specs=[anywhere] * 4,
        out_specs=(anywhere,) * 4,
        scratch_shapes=[
            pltpu.VMEM((blocks, rows, 128), kind),
            pltpu.VMEM((blocks, rows, 128), kind),
            pltpu.VMEM((per, 128, 128), kind),
            pltpu.VMEM((per, 128, 128), kind),
            dma((4, blocks)),
            dma((4,)),
            dma((2, 2, n)),
            dma((2, 2, n)),
            dma((2, chips)),
            dma((2, chips)),
            dma((2, chips, replicas)),
            dma((2, chips, replicas)),
            dma((2, chips, replicas)),
            dma((2, chips, replicas)),
        ],
        compiler_params=pltpu.CompilerParams(collective_id=0, has_side_effects=True),
        name="gather_all",
    )(activations, cotangent, up_tiles, down_tiles)


def mm(a, b, ca, cb):
    return lax.dot_general(a, b, (((ca,), (cb,)), ((), ())), preferred_element_type=jnp.float32)


def local_kernel(
    hidden_blocks, uo, uf, do, df, x, c, u, d, out, inp, ug, dg, xt, out_acc, inp_acc
):
    model_blocks = x.shape[0]

    @pl.loop(0, model_blocks)
    def _(b):
        xt[b] = x[b].T
        out_acc[b] = jnp.zeros_like(out_acc[b])
        inp_acc[b] = jnp.zeros_like(inp_acc[b])

    @pl.loop(0, hidden_blocks)
    def _(h):
        first = h * COL_TILES
        ui = [uo[first + k] for k in range(COL_TILES)]
        uj = [uf[first + k] for k in range(COL_TILES)]
        di = [do[first + k] for k in range(COL_TILES)]
        dj = [df[first + k] for k in range(COL_TILES)]
        pre = mm(x[uj[0]], u[ui[0]], 1, 0)
        hidden_grad = mm(c[dj[0]], d[di[0]], 1, 1)
        for k in range(1, COL_TILES):
            pre += mm(x[uj[k]], u[ui[k]], 1, 0)
            hidden_grad += mm(c[dj[k]], d[di[k]], 1, 1)
        value, slope = gelu_parts(pre)
        hidden = value.astype(jnp.bfloat16)
        pre_grad = (hidden_grad * slope).astype(jnp.bfloat16)
        hidden_t = hidden.T
        for k in range(COL_TILES):
            out_acc[dj[k]] += mm(hidden, d[di[k]], 1, 0)
            inp_acc[uj[k]] += mm(pre_grad, u[ui[k]], 1, 1)
            ug[ui[k]] = mm(xt[uj[k]], pre_grad, 1, 0).astype(jnp.bfloat16)
            dg[di[k]] = mm(hidden_t, c[dj[k]], 1, 0).astype(jnp.bfloat16)

    @pl.loop(0, model_blocks)
    def _(b):
        out[b] = out_acc[b].astype(jnp.bfloat16)
        inp[b] = inp_acc[b].astype(jnp.bfloat16)


def local(tables, x, c, u, d):
    vmem = pl.BlockSpec(memory_space=pltpu.VMEM)
    smem = pl.BlockSpec(memory_space=pltpu.SMEM)
    hidden_blocks = u.shape[0] // COL_TILES
    return pl.pallas_call(
        functools.partial(local_kernel, hidden_blocks),
        out_shape=tuple(jax.ShapeDtypeStruct(v.shape, jnp.bfloat16) for v in (x, x, u, u)),
        in_specs=[smem] * 4 + [vmem] * 4,
        out_specs=(vmem,) * 4,
        scratch_shapes=[
            pltpu.VMEM((x.shape[0], 128, x.shape[1]), jnp.bfloat16),
            pltpu.VMEM(x.shape, jnp.float32),
            pltpu.VMEM(x.shape, jnp.float32),
        ],
        compiler_params=pltpu.CompilerParams(vmem_limit_bytes=60 * 1024 * 1024),
        name="local_work",
    )(*tables, x, c, u, d)


def add_into(target, terms):
    @pl.loop(0, target.shape[0])
    def _(b):
        total = terms[0][b].astype(jnp.float32)
        for term in terms[1:]:
            total += term[b].astype(jnp.float32)
        target[b] = total.astype(target.dtype)


def reduce_kernel(
    sizes, out_part, inp_part, ug, dg, out, inp, ga_u, ga_d, gb_u, gb_d,
    held_r, held_l, own, core_in, x_in,
    own_sem, zs_sem, zr_sem, cs_sem, cr_sem, xs_sem, xr_sem, ys_sem, yr_sem,
):
    n, chips, replicas = sizes
    z, r, c, y = place(sizes)
    blocks = out.shape[0]
    per = ga_u.shape[0]
    size = per // PIECES
    parts = (out_part, inp_part)
    outs = (out, inp)
    grads = (ug, dg)
    sums = (ga_u, ga_d)
    others = (gb_u, gb_d)
    held = (held_r, held_l)

    def tiles(ref, r_of, c_of, k):
        return ref.at[pl.ds((r_of * 2 + c_of) * per + k * size, size)]

    def own_copy(a, k, q):
        return pltpu.make_async_copy(
            tiles(grads[a], q, c, k), own.at[a, q, pl.ds(k * size, size)], own_sem.at[a, k, q]
        )

    for a in range(2):
        for k in range(PIECES):
            for q in range(chips):
                own_copy(a, k, q).start()
    enter(sizes)

    def core_copy(a, k, q):
        return remote(
            tiles(grads[a], q, 1 - c, k), core_in.at[a, q, pl.ds(k * size, size)],
            cs_sem.at[a, k, q], cr_sem.at[a, k, q], {"fsdp": r * 2 + 1 - c},
        )

    def shard(ref, s):
        return ref.at[pl.ds(s * blocks, blocks)]

    def line(a, i, way, source):
        s = n - 1 - i if way > 0 else i
        k = 0 if way > 0 else 1
        src = shard(parts[a], s) if source else held[k].at[a, i]
        return remote(
            src, held[k].at[a, i], zs_sem.at[a, k, i], zr_sem.at[a, k, i], {"tensor": z + way}
        )

    def edge(way):
        return z == 0 if way > 0 else z == n - 1

    def sends(i, way):
        return n - 1 - i > z if way > 0 else i < z

    def keeps(i, way):
        return n - 1 - i == z if way > 0 else i == z

    def z_start():
        for i in range(n - 1):
            for a in range(2):
                for way in (1, -1):

                    @pl.when(edge(way))
                    def _():
                        line(a, i, way, True).start()

    def z_event(i, a):
        for way in (1, -1):
            s = n - 1 - i if way > 0 else i
            k = 0 if way > 0 else 1

            @pl.when(jnp.logical_and(sends(i, way), jnp.logical_not(edge(way))))
            def _():
                line(a, i, way, False).wait_recv()
                add_into(held[k].at[a, i], (held[k].at[a, i], shard(parts[a], s)))
                line(a, i, way, False).start()

    for a in range(2):
        for k in range(PIECES):
            for q in range(chips):
                core_copy(a, k, q).start()
        if a == 0:
            z_start()

    def x_copy(a, k, d):
        q = lax.rem(r + d, chips)
        return remote(
            core_in.at[a, q, pl.ds(k * size, size)], x_in.at[a, d, pl.ds(k * size, size)],
            xs_sem.at[a, k, d], xr_sem.at[a, k, d], {"fsdp": q * 2 + c},
        )

    def y_copy(a, k, e):
        return remote(
            sums[a].at[pl.ds(k * size, size)], others[a].at[e - 1, pl.ds(k * size, size)],
            ys_sem.at[a, k, e], yr_sem.at[a, k, e], {"dp": lax.rem(y + e, replicas)},
        )

    for a in range(2):
        for k in range(PIECES):
            for d in range(1, chips):
                q = lax.rem(r + d, chips)
                own_copy(a, k, q).wait()
                core_copy(a, k, q).wait_recv()
                mine = core_in.at[a, q, pl.ds(k * size, size)]
                add_into(mine, (mine, own.at[a, q, pl.ds(k * size, size)]))
                x_copy(a, k, d).start()

    def x_event(a, k):
        here = pl.ds(k * size, size)
        own_copy(a, k, r).wait()
        core_copy(a, k, r).wait_recv()
        for d in range(1, chips):
            x_copy(a, k, d).wait_recv()
        add_into(
            sums[a].at[here],
            [own.at[a, r, here], core_in.at[a, r, here]]
            + [x_in.at[a, d, here] for d in range(1, chips)],
        )
        for e in range(1, replicas):
            y_copy(a, k, e).start()

    z_events = [functools.partial(z_event, i, a) for i in range(n - 1) for a in range(2)]
    x_events = [functools.partial(x_event, a, k) for a in range(2) for k in range(PIECES)]
    for first, second in zip_longest(z_events, x_events):
        if first is not None:
            first()
        if second is not None:
            second()

    for a in range(2):
        mine = shard(parts[a], z)

        @pl.when(z > 0)
        def _():
            line(a, n - 1 - z, 1, False).wait_recv()

        @pl.when(z < n - 1)
        def _():
            line(a, z, -1, False).wait_recv()

        @pl.when(z == 0)
        def _():
            add_into(outs[a], (mine, held_l.at[a, z]))

        @pl.when(z == n - 1)
        def _():
            add_into(outs[a], (mine, held_r.at[a, n - 1 - z]))

        @pl.when(jnp.logical_and(z > 0, z < n - 1))
        def _():
            add_into(outs[a], (mine, held_r.at[a, n - 1 - z], held_l.at[a, z]))

        for i in range(n - 1):
            for way in (1, -1):

                @pl.when(sends(i, way))
                def _():
                    line(a, i, way, False).wait_send()

        for k in range(PIECES):
            for q in range(chips):
                core_copy(a, k, q).wait_send()
            for d in range(1, chips):
                x_copy(a, k, d).wait_send()
            for e in range(1, replicas):
                y_copy(a, k, e).wait()


def reduce(sizes, out_part, inp_part, ug, dg):
    n, chips, replicas = sizes
    blocks = out_part.shape[0] // n
    rows = out_part.shape[1]
    per = ug.shape[0] // (2 * chips)
    kind = jnp.bfloat16
    dma = pltpu.SemaphoreType.DMA
    vmem = pl.BlockSpec(memory_space=pltpu.VMEM)
    anywhere = pl.BlockSpec(memory_space=pl.ANY)
    return pl.pallas_call(
        functools.partial(reduce_kernel, sizes),
        out_shape=(
            [jax.ShapeDtypeStruct((blocks, rows, 128), kind)] * 2
            + [jax.ShapeDtypeStruct((per, 128, 128), kind)] * 2
            + [jax.ShapeDtypeStruct((replicas - 1, per, 128, 128), kind)] * 2
        ),
        in_specs=[vmem, vmem, anywhere, anywhere],
        out_specs=[vmem] * 4 + [anywhere] * 2,
        scratch_shapes=[
            pltpu.VMEM((2, n, blocks, rows, 128), kind),
            pltpu.VMEM((2, n, blocks, rows, 128), kind),
            pltpu.VMEM((2, chips, per, 128, 128), kind),
            pltpu.VMEM((2, chips, per, 128, 128), kind),
            pltpu.VMEM((2, chips, per, 128, 128), kind),
            dma((2, PIECES, chips)),
            dma((2, 2, n)),
            dma((2, 2, n)),
            dma((2, PIECES, chips)),
            dma((2, PIECES, chips)),
            dma((2, PIECES, chips)),
            dma((2, PIECES, chips)),
            dma((2, PIECES, replicas)),
            dma((2, PIECES, replicas)),
        ],
        compiler_params=pltpu.CompilerParams(
            collective_id=1, has_side_effects=True, vmem_limit_bytes=60 * 1024 * 1024
        ),
        name="reduce_all",
    )(out_part, inp_part, ug, dg)


def tables_of(near, far):
    count = near.shape[0]
    at = lax.iota(jnp.int32, count)
    earlier = (near[:, None] == near[None, :]) & (at[:, None] < at[None, :])
    spot = near * COL_TILES + jnp.sum(earlier.astype(jnp.int32), axis=0)
    here = spot[:, None] == at[None, :]
    order = jnp.sum(jnp.where(here, at[:, None], 0), axis=0)
    far_order = jnp.sum(jnp.where(here, far[:, None], 0), axis=0)
    return order, far_order


def body(sizes, activations, cotangent, up_tiles, down_tiles, up_rows, up_cols, down_rows, down_cols):
    up_order, up_far = tables_of(up_cols[:, 0], up_rows[:, 0])
    down_order, down_far = tables_of(down_rows[:, 0], down_cols[:, 0])
    full = gather(sizes, activations, cotangent, up_tiles, down_tiles)
    parts = local((up_order, up_far, down_order, down_far), *full)
    out, inp, ga_u, ga_d, gb_u, gb_d = reduce(sizes, *parts)

    def flat(v):
        return v.transpose(1, 0, 2).reshape(v.shape[1], -1)

    def total(a, b):
        return a.astype(jnp.float32) + jnp.sum(b.astype(jnp.float32), axis=0)

    return flat(out), flat(inp), total(ga_u, gb_u), total(ga_d, gb_d)


def solution(mesh):
    sizes = (mesh.shape["tensor"], mesh.shape["fsdp"] // 2, mesh.shape["dp"])
    in_specs = (
        P(("dp", "fsdp"), "tensor"),
        P(("dp", "fsdp"), "tensor"),
        P(("fsdp", "tensor"), None, None),
        P(("fsdp", "tensor"), None, None),
        P(None, "tensor"),
        P(None, "tensor"),
        P(None, "tensor"),
        P(None, "tensor"),
    )
    out_specs = (
        P(("dp", "fsdp"), "tensor"),
        P(("dp", "fsdp"), "tensor"),
        P(("fsdp", "tensor"), None, None),
        P(("fsdp", "tensor"), None, None),
    )
    return jax.shard_map(
        functools.partial(body, sizes), mesh=mesh, in_specs=in_specs, out_specs=out_specs,
        check_vma=False,
    )
```

time: 593 us -> 295 us (0.50); the launches traced: 582 us -> 295 us
  Pallas kernels: 0 us -> 279 us
  waiting for transfers between devices: 217 us -> 0 us
  local copies, waits for them, and re-layouts: 157 us -> 3.78 us
  other arithmetic: 131 us -> 11.9 us
  matrix products: 61.1 us -> 0 us
  between operations: 14.8 us -> 0.68 us
    pallas_call x0 -> x3, Pallas kernels: none -> 279 us  [the longest x1 151 us: reduce(): pl.pallas_call(functools.partial(reduce_kernel, sizes), out_shape=[jax.Sh...]
    all_gather x6 -> x0, waiting for transfers between devices: 173 us -> none  [the longest x1 43.1 us: body(): full_cotangent = lax.all_gather(cotangent, 'tensor', axis=1, tiled=True)]
    scatter-add x2 -> x0, other arithmetic: 104 us -> none  [add_far(): jnp.zeros((rows_here, model_blocks, block_size), jnp.float32)]
    gather x8 -> x0, local copies, waits for them, and re-layouts: 73.5 us -> none  [the longest x2 25.6 us: grouped_tiles(): return tiles[order].reshape(hidden_blocks, -1, block_size, block_size)]
    dot_general x6 -> x0, matrix products: 61.1 us -> none  [the longest x1 11.6 us: body(): jnp.einsum('thb,hkbc->thkc', hidden, down_sorted, preferred_element_type=...]
    reshape x4 -> x0, local copies, waits for them, and re-layouts: 42.3 us -> none  [the longest x2 35 us: add_far(): flat = product.reshape(rows_here, -1, block_size)]
    reduce_scatter x4 -> x0, waiting for transfers between devices: 40.9 us -> none  [the longest x1 40.8 us: body(): lax.psum_scatter(partial_in.astype(jnp.bfloat16), 'tensor', scatter_dimen...]
    convert_element_type x4 -> x0, local copies, waits for them, and re-layouts: 28.2 us -> none  [the longest x1 12 us: body(): regroup(down_term).astype(jnp.bfloat16)]
  transfers between devices with their start and end apart: 10 -> 0, of which waited for: 7 -> 0; matrix products, arithmetic and copies ran while one was open for 59% -> 0% of each run, Pallas kernels for 0% -> 0%
where the time goes in v1:
time: 295 us
  Pallas kernels  279 us (95%)
  other arithmetic  11.9 us (4%)
  local copies, waits for them, and re-layouts  3.78 us (1%)
    pallas_call x1, Pallas kernels, reduce(): pl.pallas_call(functools.partial(reduce_kernel, sizes), out_shape=[jax.Sh...  151 us
    pallas_call x1, Pallas kernels, gather(): pl.pallas_call(functools.partial(gather_kernel, sizes), out_shape=(jax.Sh...  76.9 us
    pallas_call x1, Pallas kernels, local(): pl.pallas_call(functools.partial(local_kernel, hidden_blocks), out_shape=...  50.6 us
    add x2, other arithmetic, total(): return a.astype(jnp.float32) + jnp.sum(b.astype(jnp.float32), axis=0)  7.33 us

profile of v1, /device:TPU:8, one launch (start us, length us, event | category | flops | bytes accessed | tf_op | source)
XLA Modules:
  0.0 295.1 jit_solution(14712461875221350601)
XLA Ops:
  0.6 0.9 convert_reduce_fusion
  1.5 0.7 multiply_add_fusion
  2.2 0.9 convert_reduce_fusion.1
  3.1 0.7 multiply_add_fusion.1
  3.7 1.5 select_reduce_fusion
  5.2 76.9 %gather_all.1 = (bf16[64,128,128]{2,1,0:T(8,128)(2,1)}, bf16[64,128,128]{2,1,0:T(8,128)(2,1)}, bf16[256,128,128]{2,1,0:T(8,128)(2,1)}, bf16[256,128,128]{2,1,0:T(8,128)(2,1)}) custom-call(bf16[128,2048]{1,0:T(8,128)(2,1)} %act.1, bf16[128,2048]{1,0:T(8,128)(2,1)} %cot.1, bf16[64,128,128]{2,1,0:T(8,128)(2,1)} %up.1, bf16[64,128,128]{2,1,0:T(8,128)(2,1)} %down.1), custom_call_target="tpu_custom_call" | custom-call | tf_op jit(solution)/shard_map/gather_all/pallas_call | solution.py:233
  82.1 50.6 %local_work.1 = (bf16[64,128,128]{2,1,0:T(8,128)(2,1)}, bf16[64,128,128]{2,1,0:T(8,128)(2,1)}, bf16[256,128,128]{2,1,0:T(8,128)(2,1)}, bf16[256,128,128]{2,1,0:T(8,128)(2,1)}) custom-call(s32[256]{0:T(256)} %get-tuple-element.44.uo, s32[256]{0:T(256)} %get-tuple-element.45.uf, s32[256]{0:T(256)} %get-tuple-element.41.do, s32[256]{0:T(256)} %get-tuple-element.40.df, ...), custom_call_target="tpu_custom_call" | custom-call | tf_op jit(solution)/shard_map/local_work/pallas_call | solution.py:311
  132.7 151.3 %reduce_all.1 = (bf16[16,128,128]{2,1,0:T(8,128)(2,1)}, bf16[16,128,128]{2,1,0:T(8,128)(2,1)}, bf16[64,128,128]{2,1,0:T(8,128)(2,1)}, bf16[64,128,128]{2,1,0:T(8...) custom-call(bf16[64,128,128]{2,1,0:T(8,128)(2,1)} %get-tuple-element.22.out_part, ...), custom_call_target="tpu_custom_call" | custom-call | tf_op jit(solution)/shard_map/reduce_all/pallas_call | solution.py:512
  284.0 0.0 copy-start.3
  284.0 0.0 copy-start.2
  284.0 1.5 copy.16
  285.5 1.0 copy.18
  286.5 0.0 copy-done.3
  286.5 0.3 copy.17
  286.8 1.0 copy.19
  287.8 0.0 copy-done.2
  287.8 0.0 copy-start
  287.8 0.0 copy-start.1
  287.8 4.5 %convert_add_fusion.1 = f32[64,128,128]{2,1,0:T(8,128)} fusion(bf16[64,128,128]{2,1,0:T(8,128)(2,1)S(1)} %copy-done.2, bf16[1,64,128,128]{3,2,1,0:T(8,128)(2,1)} %get-tuple-element.29), kind=kLoop, calls=%fused_computation.1 | loop fusion | flops 3145728 | bytes 8388608 | tf_op jit(solution)/shard_map/add | solution.py:566
  292.3 0.0 copy-done
  292.3 0.0 copy-done.1
  292.3 2.8 convert_add_fusion
Async XLA Ops:
  284.0 2.5 copy-start.3
  284.0 3.8 %copy-start.2 = (bf16[64,128,128]{2,1,0:T(8,128)(2,1)S(1)}, bf16[64,128,128]{2,1,0:T(8,128)(2,1)}, u32[]{:S(2)}) copy-start(bf16[64,128,128]{2,1,0:T(8,128)(2,1)} %get-tuple-element.28) | copy-start | bytes 6291460
  287.8 4.5 %copy-start = (bf16[64,128,128]{2,1,0:T(8,128)(2,1)S(1)}, bf16[64,128,128]{2,1,0:T(8,128)(2,1)}, u32[]{:S(2)}) copy-start(bf16[64,128,128]{2,1,0:T(8,128)(2,1)} %get-tuple-element.30) | copy-start | bytes 6291460
  287.8 4.5 %copy-start.1 = (bf16[1,64,128,128]{3,2,1,0:T(8,128)(2,1)S(1)}, bf16[1,64,128,128]{3,2,1,0:T(8,128)(2,1)}, u32[]{:S(2)}) copy-start(bf16[1,64,128,128]{3,2,1,0:T(8,128)(2,1)} %get-tuple-element.31) | copy-start | bytes 6291460

commit v2 on v1

--- a/solution.py
+++ b/solution.py
@@ -10,7 +10,8 @@
 
 MESH = pl.DeviceIdType.MESH
 COL_TILES = 8
-PIECES = 4
+PIECES = 8
+AHEAD = 4
 
 inv_root_two = 0.7071067811865476
 inv_root_tau = 0.3989422804014327
@@ -398,12 +399,14 @@
                     def _():
                         line(a, i, way, True).start()
 
-    def z_event(i, a):
+    def z_event(t, a):
         for way in (1, -1):
+            i = t - z if way > 0 else t - (n - 1 - z)
             s = n - 1 - i if way > 0 else i
             k = 0 if way > 0 else 1
-
-            @pl.when(jnp.logical_and(sends(i, way), jnp.logical_not(edge(way))))
+            on_way = jnp.logical_and(i >= 0, sends(i, way))
+
+            @pl.when(jnp.logical_and(on_way, jnp.logical_not(edge(way))))
             def _():
                 line(a, i, way, False).wait_recv()
                 add_into(held[k].at[a, i], (held[k].at[a, i], shard(parts[a], s)))
@@ -429,15 +432,14 @@
             ys_sem.at[a, k, e], yr_sem.at[a, k, e], {"dp": lax.rem(y + e, replicas)},
         )
 
-    for a in range(2):
-        for k in range(PIECES):
-            for d in range(1, chips):
-                q = lax.rem(r + d, chips)
-                own_copy(a, k, q).wait()
-                core_copy(a, k, q).wait_recv()
-                mine = core_in.at[a, q, pl.ds(k * size, size)]
-                add_into(mine, (mine, own.at[a, q, pl.ds(k * size, size)]))
-                x_copy(a, k, d).start()
+    def feed(a, k):
+        for d in range(1, chips):
+            q = lax.rem(r + d, chips)
+            own_copy(a, k, q).wait()
+            core_copy(a, k, q).wait_recv()
+            mine = core_in.at[a, q, pl.ds(k * size, size)]
+            add_into(mine, (mine, own.at[a, q, pl.ds(k * size, size)]))
+            x_copy(a, k, d).start()
 
     def x_event(a, k):
         here = pl.ds(k * size, size)
@@ -453,13 +455,18 @@
         for e in range(1, replicas):
             y_copy(a, k, e).start()
 
-    z_events = [functools.partial(z_event, i, a) for i in range(n - 1) for a in range(2)]
-    x_events = [functools.partial(x_event, a, k) for a in range(2) for k in range(PIECES)]
-    for first, second in zip_longest(z_events, x_events):
-        if first is not None:
-            first()
-        if second is not None:
-            second()
+    pieces = [(a, k) for a in range(2) for k in range(PIECES)]
+    slots = [(t, a) for t in range(1, n - 1) for a in range(2)]
+    for piece in pieces[:AHEAD]:
+        feed(*piece)
+    for i, piece in enumerate(pieces):
+        if i % 2 == 0 and i >= 2 and slots:
+            z_event(*slots.pop(0))
+        if i + AHEAD < len(pieces):
+            feed(*pieces[i + AHEAD])
+        x_event(*piece)
+    for slot in slots:
+        z_event(*slot)
 
     for a in range(2):
         mine = shard(parts[a], z)

time: 295 us -> 255 us (0.86)
  Pallas kernels: 279 us -> 237 us
    pallas_call x1, Pallas kernels: 151 us -> 109 us  [reduce(): pl.pallas_call(functools.partial(reduce_kernel, sizes), out_shape=[jax.Sh...]
where the time goes in v2:
time: 255 us; the launch traced here: 253 us
  Pallas kernels  237 us (93%)
  other arithmetic  11.9 us (5%)
  local copies, waits for them, and re-layouts  3.78 us (1%)
    pallas_call x1, Pallas kernels, reduce(): pl.pallas_call(functools.partial(reduce_kernel, sizes), out_shape=[jax.Sh...  109 us
    pallas_call x1, Pallas kernels, gather(): pl.pallas_call(functools.partial(gather_kernel, sizes), out_shape=(jax.Sh...  76.9 us
    pallas_call x1, Pallas kernels, local(): pl.pallas_call(functools.partial(local_kernel, hidden_blocks), out_shape=...  50.6 us
    add x2, other arithmetic, total(): return a.astype(jnp.float32) + jnp.sum(b.astype(jnp.float32), axis=0)  7.33 us

profile of v2, /device:TPU:8, one launch (start us, length us, event | category | flops | bytes accessed | tf_op | source)
XLA Modules:
  0.0 253.3 jit_solution(5397632415208148395)
XLA Ops:
  0.6 0.9 convert_reduce_fusion
  1.5 0.7 multiply_add_fusion
  2.2 0.9 convert_reduce_fusion.1
  3.1 0.7 multiply_add_fusion.1
  3.7 1.5 select_reduce_fusion
  5.2 76.9 %gather_all.1 = (bf16[64,128,128]{2,1,0:T(8,128)(2,1)}, bf16[64,128,128]{2,1,0:T(8,128)(2,1)}, bf16[256,128,128]{2,1,0:T(8,128)(2,1)}, bf16[256,128,128]{2,1,0:T(8,128)(2,1)}) custom-call(bf16[128,2048]{1,0:T(8,128)(2,1)} %act.1, bf16[128,2048]{1,0:T(8,128)(2,1)} %cot.1, bf16[64,128,128]{2,1,0:T(8,128)(2,1)} %up.1, bf16[64,128,128]{2,1,0:T(8,128)(2,1)} %down.1), custom_call_target="tpu_custom_call" | custom-call | tf_op jit(solution)/shard_map/gather_all/pallas_call | solution.py:234
  82.1 50.6 %local_work.1 = (bf16[64,128,128]{2,1,0:T(8,128)(2,1)}, bf16[64,128,128]{2,1,0:T(8,128)(2,1)}, bf16[256,128,128]{2,1,0:T(8,128)(2,1)}, bf16[256,128,128]{2,1,0:T(8,128)(2,1)}) custom-call(s32[256]{0:T(256)} %get-tuple-element.44.uo, s32[256]{0:T(256)} %get-tuple-element.45.uf, s32[256]{0:T(256)} %get-tuple-element.41.do, s32[256]{0:T(256)} %get-tuple-element.40.df, ...), custom_call_target="tpu_custom_call" | custom-call | tf_op jit(solution)/shard_map/local_work/pallas_call | solution.py:312
  132.7 109.4 %reduce_all.1 = (bf16[16,128,128]{2,1,0:T(8,128)(2,1)}, bf16[16,128,128]{2,1,0:T(8,128)(2,1)}, bf16[64,128,128]{2,1,0:T(8,128)(2,1)}, bf16[64,128,128]{2,1,0:T(8...) custom-call(bf16[64,128,128]{2,1,0:T(8,128)(2,1)} %get-tuple-element.22.out_part, ...), custom_call_target="tpu_custom_call" | custom-call | tf_op jit(solution)/shard_map/reduce_all/pallas_call | solution.py:519
  242.1 0.0 copy-start.3
  242.1 0.0 copy-start.2
  242.1 1.5 copy.16
  243.6 1.0 copy.18
  244.6 0.0 copy-done.3
  244.6 0.3 copy.17
  244.9 1.0 copy.19
  245.9 0.0 copy-done.2
  245.9 0.0 copy-start
  245.9 0.0 copy-start.1
  245.9 4.5 %convert_add_fusion.1 = f32[64,128,128]{2,1,0:T(8,128)} fusion(bf16[64,128,128]{2,1,0:T(8,128)(2,1)S(1)} %copy-done.2, bf16[1,64,128,128]{3,2,1,0:T(8,128)(2,1)} %get-tuple-element.29), kind=kLoop, calls=%fused_computation.1 | loop fusion | flops 3145728 | bytes 8388608 | tf_op jit(solution)/shard_map/add | solution.py:573
  250.4 0.0 copy-done
  250.4 0.0 copy-done.1
  250.4 2.8 %convert_add_fusion = f32[64,128,128]{2,1,0:T(8,128)} fusion(bf16[64,128,128]{2,1,0:T(8,128)(2,1)S(1)} %copy-done, bf16[1,64,128,128]{3,2,1,0:T(8,128)(2,1)S(1)} %copy-done.1), kind=kLoop, calls=%fused_computation | loop fusion | flops 3145728 | bytes 8388608 | tf_op jit(solution)/shard_map/add | solution.py:573
Async XLA Ops:
  242.1 2.5 copy-start.3
  242.1 3.8 %copy-start.2 = (bf16[64,128,128]{2,1,0:T(8,128)(2,1)S(1)}, bf16[64,128,128]{2,1,0:T(8,128)(2,1)}, u32[]{:S(2)}) copy-start(bf16[64,128,128]{2,1,0:T(8,128)(2,1)} %get-tuple-element.28) | copy-start | bytes 6291460
  245.9 4.5 %copy-start = (bf16[64,128,128]{2,1,0:T(8,128)(2,1)S(1)}, bf16[64,128,128]{2,1,0:T(8,128)(2,1)}, u32[]{:S(2)}) copy-start(bf16[64,128,128]{2,1,0:T(8,128)(2,1)} %get-tuple-element.30) | copy-start | bytes 6291460
  245.9 4.5 %copy-start.1 = (bf16[1,64,128,128]{3,2,1,0:T(8,128)(2,1)S(1)}, bf16[1,64,128,128]{3,2,1,0:T(8,128)(2,1)}, u32[]{:S(2)}) copy-start(bf16[1,64,128,128]{3,2,1,0:T(8,128)(2,1)} %get-tuple-element.31) | copy-start | bytes 6291460

commit v3 on v2

--- a/solution.py
+++ b/solution.py
@@ -11,7 +11,6 @@
 MESH = pl.DeviceIdType.MESH
 COL_TILES = 8
 PIECES = 8
-AHEAD = 4
 
 inv_root_two = 0.7071067811865476
 inv_root_tau = 0.3989422804014327
@@ -266,62 +265,39 @@
     return lax.dot_general(a, b, (((ca,), (cb,)), ((), ())), preferred_element_type=jnp.float32)
 
 
-def local_kernel(
-    hidden_blocks, uo, uf, do, df, x, c, u, d, out, inp, ug, dg, xt, out_acc, inp_acc
-):
-    model_blocks = x.shape[0]
-
-    @pl.loop(0, model_blocks)
+def forward_kernel(hidden_blocks, uo, uf, x, u, hidden, slope, xt):
+    @pl.loop(0, x.shape[0])
     def _(b):
         xt[b] = x[b].T
-        out_acc[b] = jnp.zeros_like(out_acc[b])
-        inp_acc[b] = jnp.zeros_like(inp_acc[b])
 
     @pl.loop(0, hidden_blocks)
     def _(h):
         first = h * COL_TILES
-        ui = [uo[first + k] for k in range(COL_TILES)]
-        uj = [uf[first + k] for k in range(COL_TILES)]
-        di = [do[first + k] for k in range(COL_TILES)]
-        dj = [df[first + k] for k in range(COL_TILES)]
-        pre = mm(x[uj[0]], u[ui[0]], 1, 0)
-        hidden_grad = mm(c[dj[0]], d[di[0]], 1, 1)
+        pre = mm(x[uf[first]], u[uo[first]], 1, 0)
         for k in range(1, COL_TILES):
-            pre += mm(x[uj[k]], u[ui[k]], 1, 0)
-            hidden_grad += mm(c[dj[k]], d[di[k]], 1, 1)
-        value, slope = gelu_parts(pre)
-        hidden = value.astype(jnp.bfloat16)
-        pre_grad = (hidden_grad * slope).astype(jnp.bfloat16)
-        hidden_t = hidden.T
-        for k in range(COL_TILES):
-            out_acc[dj[k]] += mm(hidden, d[di[k]], 1, 0)
-            inp_acc[uj[k]] += mm(pre_grad, u[ui[k]], 1, 1)
-            ug[ui[k]] = mm(xt[uj[k]], pre_grad, 1, 0).astype(jnp.bfloat16)
-            dg[di[k]] = mm(hidden_t, c[dj[k]], 1, 0).astype(jnp.bfloat16)
-
-    @pl.loop(0, model_blocks)
-    def _(b):
-        out[b] = out_acc[b].astype(jnp.bfloat16)
-        inp[b] = inp_acc[b].astype(jnp.bfloat16)
-
-
-def local(tables, x, c, u, d):
+            pre += mm(x[uf[first + k]], u[uo[first + k]], 1, 0)
+        value, tangent = gelu_parts(pre)
+        hidden[h] = value.astype(jnp.bfloat16)
+        slope[h] = tangent
+
+
+def forward(order, far, x, u):
     vmem = pl.BlockSpec(memory_space=pltpu.VMEM)
     smem = pl.BlockSpec(memory_space=pltpu.SMEM)
     hidden_blocks = u.shape[0] // COL_TILES
+    rows = x.shape[1]
     return pl.pallas_call(
-        functools.partial(local_kernel, hidden_blocks),
-        out_shape=tuple(jax.ShapeDtypeStruct(v.shape, jnp.bfloat16) for v in (x, x, u, u)),
-        in_specs=[smem] * 4 + [vmem] * 4,
-        out_specs=(vmem,) * 4,
-        scratch_shapes=[
-            pltpu.VMEM((x.shape[0], 128, x.shape[1]), jnp.bfloat16),
-            pltpu.VMEM(x.shape, jnp.float32),
-            pltpu.VMEM(x.shape, jnp.float32),
-        ],
+        functools.partial(forward_kernel, hidden_blocks),
+        out_shape=(
+            jax.ShapeDtypeStruct((hidden_blocks, rows, 128), jnp.bfloat16),
+            jax.ShapeDtypeStruct((hidden_blocks, rows, 128), jnp.float32),
+            jax.ShapeDtypeStruct((x.shape[0], 128, rows), jnp.bfloat16),
+        ),
+        in_specs=[smem] * 2 + [vmem] * 2,
+        out_specs=(vmem,) * 3,
         compiler_params=pltpu.CompilerParams(vmem_limit_bytes=60 * 1024 * 1024),
-        name="local_work",
-    )(*tables, x, c, u, d)
+        name="forward_work",
+    )(order, far, x, u)
 
 
 def add_into(target, terms):
@@ -334,41 +310,121 @@
 
 
 def reduce_kernel(
-    sizes, out_part, inp_part, ug, dg, out, inp, ga_u, ga_d, gb_u, gb_d,
-    held_r, held_l, own, core_in, x_in,
-    own_sem, zs_sem, zr_sem, cs_sem, cr_sem, xs_sem, xr_sem, ys_sem, yr_sem,
+    sizes, do, df, up_rows, up_cols, down_rows, down_cols,
+    far_order_u, far_near_u, far_first_u, last_u, far_order_d, far_near_d, far_first_d, last_d,
+    hidden, slope, xt, cot, up, down,
+    out, inp, ga_u, ga_d, gb_u, gb_d,
+    u_all, d_all, hidden_t, pre_grad, run, acc, parts_o, parts_i,
+    held_r, held_l, stage, core_in, x_in,
+    load_sem, keep_sem, zs_sem, zr_sem, cs_sem, cr_sem, xs_sem, xr_sem, ys_sem, yr_sem,
 ):
     n, chips, replicas = sizes
     z, r, c, y = place(sizes)
     blocks = out.shape[0]
+    hidden_blocks = hidden.shape[0]
     per = ga_u.shape[0]
+    total_tiles = u_all.shape[0]
     size = per // PIECES
-    parts = (out_part, inp_part)
+    parts = (parts_o, parts_i)
     outs = (out, inp)
-    grads = (ug, dg)
-    sums = (ga_u, ga_d)
-    others = (gb_u, gb_d)
+    sums = (ga_d, ga_u)
+    others = (gb_d, gb_u)
     held = (held_r, held_l)
 
-    def tiles(ref, r_of, c_of, k):
-        return ref.at[pl.ds((r_of * 2 + c_of) * per + k * size, size)]
-
-    def own_copy(a, k, q):
+    load_d = pltpu.make_async_copy(down, d_all, load_sem.at[0])
+    load_u = pltpu.make_async_copy(up, u_all, load_sem.at[1])
+    load_d.start()
+    load_u.start()
+    enter(sizes)
+
+    @pl.loop(0, hidden_blocks)
+    def _(h):
+        hidden_t[h] = hidden[h].T
+
+    def term(a, j):
+        if a == 0:
+            return mm(hidden_t[down_rows[j]], cot[down_cols[j]], 1, 0)
+        return mm(xt[up_rows[j]], pre_grad[up_cols[j]], 1, 0)
+
+    def first_tile(q, c_of, k):
+        return (q * 2 + c_of) * per + k * size
+
+    width = 4 if size % 4 == 0 else 1
+
+    def staged(a, k, q):
+        at = (k * chips + q) * size
+        return (stage if a == 0 else d_all).at[pl.ds(at, size)]
+
+    def core_copy(a, k, q):
+        return remote(
+            staged(a, k, q), core_in.at[a, q, pl.ds(k * size, size)],
+            cs_sem.at[a, k, q], cr_sem.at[a, k, q], {"fsdp": r * 2 + 1 - c},
+        )
+
+    def hand_over(a, k):
+        for q in range(chips):
+            target = staged(a, k, q)
+
+            @pl.loop(0, size // width)
+            def _(i):
+                values = [term(a, first_tile(q, 1 - c, k) + i * width + w) for w in range(width)]
+                for w in range(width):
+                    target[i * width + w] = values[w].astype(jnp.bfloat16)
+
+        for q in range(chips):
+            core_copy(a, k, q).start()
+
+    def sum_with(a, k, q, target, terms):
+        @pl.loop(0, size // width)
+        def _(i):
+            values = [term(a, first_tile(q, c, k) + i * width + w) for w in range(width)]
+            for w in range(width):
+                total = values[w].astype(jnp.bfloat16).astype(jnp.float32)
+                for other in terms:
+                    total += other[i * width + w].astype(jnp.float32)
+                target[i * width + w] = total.astype(jnp.bfloat16)
+
+    def x_copy(a, k, d):
+        q = lax.rem(r + d, chips)
+        return remote(
+            core_in.at[a, q, pl.ds(k * size, size)], x_in.at[a, d - 1, pl.ds(k * size, size)],
+            xs_sem.at[a, k, d], xr_sem.at[a, k, d], {"fsdp": q * 2 + c},
+        )
+
+    def done_piece(a, k):
+        return core_in.at[a, r, pl.ds(k * size, size)]
+
+    def y_copy(a, k, e):
+        return remote(
+            done_piece(a, k), others[a].at[e - 1, pl.ds(k * size, size)],
+            ys_sem.at[a, k, e], yr_sem.at[a, k, e], {"dp": lax.rem(y + e, replicas)},
+        )
+
+    def keep_copy(a, k):
         return pltpu.make_async_copy(
-            tiles(grads[a], q, c, k), own.at[a, q, pl.ds(k * size, size)], own_sem.at[a, k, q]
-        )
-
-    for a in range(2):
-        for k in range(PIECES):
-            for q in range(chips):
-                own_copy(a, k, q).start()
-    enter(sizes)
-
-    def core_copy(a, k, q):
-        return remote(
-            tiles(grads[a], q, 1 - c, k), core_in.at[a, q, pl.ds(k * size, size)],
-            cs_sem.at[a, k, q], cr_sem.at[a, k, q], {"fsdp": r * 2 + 1 - c},
-        )
+            done_piece(a, k), sums[a].at[pl.ds(k * size, size)], keep_sem.at[a, k]
+        )
+
+    def feed(a, k):
+        for d in range(1, chips):
+            q = lax.rem(r + d, chips)
+            core_copy(a, k, q).wait_recv()
+            mine = core_in.at[a, q, pl.ds(k * size, size)]
+            sum_with(a, k, q, mine, [mine])
+            x_copy(a, k, d).start()
+
+    def x_event(a, k):
+        core_copy(a, k, r).wait_recv()
+        for d in range(1, chips):
+            x_copy(a, k, d).wait_recv()
+        mine = done_piece(a, k)
+        sum_with(
+            a, k, r, mine,
+            [mine] + [x_in.at[a, d - 1, pl.ds(k * size, size)] for d in range(1, chips)],
+        )
+        for e in range(1, replicas):
+            y_copy(a, k, e).start()
+        keep_copy(a, k).start()
 
     def shard(ref, s):
         return ref.at[pl.ds(s * blocks, blocks)]
@@ -387,17 +443,13 @@
     def sends(i, way):
         return n - 1 - i > z if way > 0 else i < z
 
-    def keeps(i, way):
-        return n - 1 - i == z if way > 0 else i == z
-
-    def z_start():
+    def z_start(a):
         for i in range(n - 1):
-            for a in range(2):
-                for way in (1, -1):
-
-                    @pl.when(edge(way))
-                    def _():
-                        line(a, i, way, True).start()
+            for way in (1, -1):
+
+                @pl.when(edge(way))
+                def _():
+                    line(a, i, way, True).start()
 
     def z_event(t, a):
         for way in (1, -1):
@@ -412,58 +464,84 @@
                 add_into(held[k].at[a, i], (held[k].at[a, i], shard(parts[a], s)))
                 line(a, i, way, False).start()
 
-    for a in range(2):
-        for k in range(PIECES):
-            for q in range(chips):
-                core_copy(a, k, q).start()
-        if a == 0:
-            z_start()
-
-    def x_copy(a, k, d):
-        q = lax.rem(r + d, chips)
-        return remote(
-            core_in.at[a, q, pl.ds(k * size, size)], x_in.at[a, d, pl.ds(k * size, size)],
-            xs_sem.at[a, k, d], xr_sem.at[a, k, d], {"fsdp": q * 2 + c},
-        )
-
-    def y_copy(a, k, e):
-        return remote(
-            sums[a].at[pl.ds(k * size, size)], others[a].at[e - 1, pl.ds(k * size, size)],
-            ys_sem.at[a, k, e], yr_sem.at[a, k, e], {"dp": lax.rem(y + e, replicas)},
-        )
-
-    def feed(a, k):
-        for d in range(1, chips):
-            q = lax.rem(r + d, chips)
-            own_copy(a, k, q).wait()
-            core_copy(a, k, q).wait_recv()
-            mine = core_in.at[a, q, pl.ds(k * size, size)]
-            add_into(mine, (mine, own.at[a, q, pl.ds(k * size, size)]))
-            x_copy(a, k, d).start()
-
-    def x_event(a, k):
-        here = pl.ds(k * size, size)
-        own_copy(a, k, r).wait()
-        core_copy(a, k, r).wait_recv()
-        for d in range(1, chips):
-            x_copy(a, k, d).wait_recv()
-        add_into(
-            sums[a].at[here],
-            [own.at[a, r, here], core_in.at[a, r, here]]
-            + [x_in.at[a, d, here] for d in range(1, chips)],
-        )
-        for e in range(1, replicas):
-            y_copy(a, k, e).start()
-
+    def slope_part(g):
+        span = hidden_blocks // 4
+
+        @pl.loop(g * span, (g + 1) * span)
+        def _(h):
+            first = h * COL_TILES
+            value = mm(cot[df[first]], d_all[do[first]], 1, 1)
+            for k in range(1, COL_TILES):
+                value += mm(cot[df[first + k]], d_all[do[first + k]], 1, 1)
+            pre_grad[h] = (value * slope[h]).astype(jnp.bfloat16)
+
+    def run_part(a, g):
+        order, near, fresh = (
+            (far_order_d, far_near_d, far_first_d) if a == 0 else (far_order_u, far_near_u, far_first_u)
+        )
+        left, right, cut = (hidden, d_all, 0) if a == 0 else (pre_grad, u_all, 1)
+        span = total_tiles // 4 // 8
+        if g == 0:
+            acc[...] = jnp.zeros_like(acc)
+
+        @pl.loop(g * span, (g + 1) * span)
+        def _(b):
+            spots = [b * 8 + k for k in range(8)]
+            products = [mm(left[near[i]], right[order[i]], 1, cut) for i in spots]
+            total = acc[...]
+            for i, product in zip(spots, products):
+                total = jnp.where(fresh[i] == 1, 0.0, total) + product
+                run[i] = total.astype(jnp.bfloat16)
+            acc[...] = total
+
+    def settle(a):
+        last = last_d if a == 0 else last_u
+        target = parts[a]
+
+        @pl.loop(0, target.shape[0])
+        def _(b):
+            spot = last[b]
+            found = run[jnp.maximum(spot, 0)]
+            target[b] = jnp.where(spot >= 0, found, jnp.zeros_like(found))
+
+        z_start(a)
+
+    for k in range(PIECES):
+        hand_over(0, k)
+    for k in range(PIECES):
+        feed(0, k)
+    load_d.wait()
+    load_u.wait()
+    work = (
+        [functools.partial(slope_part, g) for g in range(4)]
+        + [functools.partial(run_part, 0, g) for g in range(4)]
+        + [functools.partial(settle, 0)]
+        + [functools.partial(run_part, 1, g) for g in range(4)]
+        + [functools.partial(settle, 1)]
+    )
+    slots = [(t, a) for a in range(2) for t in range(1, n - 1)]
     pieces = [(a, k) for a in range(2) for k in range(PIECES)]
-    slots = [(t, a) for t in range(1, n - 1) for a in range(2)]
-    for piece in pieces[:AHEAD]:
-        feed(*piece)
+    handed = 0
+    fed = 0
     for i, piece in enumerate(pieces):
-        if i % 2 == 0 and i >= 2 and slots:
+        for step in work[:3]:
+            step()
+        work = work[3:]
+        if not work and handed < PIECES:
+            hand_over(1, handed)
+            handed += 1
+        if not work and handed >= 2 and fed < handed - 1:
+            feed(1, fed)
+            fed += 1
+        if i >= 5 and i % 2 == 1 and slots:
             z_event(*slots.pop(0))
-        if i + AHEAD < len(pieces):
-            feed(*pieces[i + AHEAD])
+        if i == PIECES - 1:
+            while handed < PIECES:
+                hand_over(1, handed)
+                handed += 1
+        if i >= PIECES - 1 and fed < PIECES:
+            feed(1, fed)
+            fed += 1
         x_event(*piece)
     for slot in slots:
         z_event(*slot)
@@ -503,18 +581,20 @@
                 core_copy(a, k, q).wait_send()
             for d in range(1, chips):
                 x_copy(a, k, d).wait_send()
+            keep_copy(a, k).wait()
             for e in range(1, replicas):
                 y_copy(a, k, e).wait()
 
 
-def reduce(sizes, out_part, inp_part, ug, dg):
+def reduce(sizes, tables, hidden, slope, xt, cot, up, down):
     n, chips, replicas = sizes
-    blocks = out_part.shape[0] // n
-    rows = out_part.shape[1]
-    per = ug.shape[0] // (2 * chips)
+    blocks = cot.shape[0] // n
+    rows = cot.shape[1]
+    per = up.shape[0] // (2 * chips)
     kind = jnp.bfloat16
     dma = pltpu.SemaphoreType.DMA
     vmem = pl.BlockSpec(memory_space=pltpu.VMEM)
+    smem = pl.BlockSpec(memory_space=pltpu.SMEM)
     anywhere = pl.BlockSpec(memory_space=pl.ANY)
     return pl.pallas_call(
         functools.partial(reduce_kernel, sizes),
@@ -523,15 +603,24 @@
             + [jax.ShapeDtypeStruct((per, 128, 128), kind)] * 2
             + [jax.ShapeDtypeStruct((replicas - 1, per, 128, 128), kind)] * 2
         ),
-        in_specs=[vmem, vmem, anywhere, anywhere],
-        out_specs=[vmem] * 4 + [anywhere] * 2,
+        in_specs=[smem] * len(tables) + [vmem] * 4 + [anywhere] * 2,
+        out_specs=[vmem] * 2 + [anywhere] * 4,
         scratch_shapes=[
-            pltpu.VMEM((2, n, blocks, rows, 128), kind),
-            pltpu.VMEM((2, n, blocks, rows, 128), kind),
+            pltpu.VMEM(up.shape, kind),
+            pltpu.VMEM(down.shape, kind),
+            pltpu.VMEM((hidden.shape[0], 128, rows), kind),
+            pltpu.VMEM(hidden.shape, kind),
+            pltpu.VMEM((up.shape[0], rows, 128), kind),
+            pltpu.VMEM((rows, 128), jnp.float32),
+            pltpu.VMEM(cot.shape, kind),
+            pltpu.VMEM(cot.shape, kind),
+            pltpu.VMEM((2, n - 1, blocks, rows, 128), kind),
+            pltpu.VMEM((2, n - 1, blocks, rows, 128), kind),
+            pltpu.VMEM((chips * per, 128, 128), kind),
             pltpu.VMEM((2, chips, per, 128, 128), kind),
-            pltpu.VMEM((2, chips, per, 128, 128), kind),
-            pltpu.VMEM((2, chips, per, 128, 128), kind),
-            dma((2, PIECES, chips)),
+            pltpu.VMEM((2, max(chips - 1, 1), per, 128, 128), kind),
+            dma((2,)),
+            dma((2, PIECES)),
             dma((2, 2, n)),
             dma((2, 2, n)),
             dma((2, PIECES, chips)),
@@ -542,29 +631,49 @@
             dma((2, PIECES, replicas)),
         ],
         compiler_params=pltpu.CompilerParams(
-            collective_id=1, has_side_effects=True, vmem_limit_bytes=60 * 1024 * 1024
+            collective_id=1, has_side_effects=True, vmem_limit_bytes=67043328
         ),
         name="reduce_all",
-    )(out_part, inp_part, ug, dg)
-
-
-def tables_of(near, far):
+    )(*tables, hidden, slope, xt, cot, up, down)
+
+
+def tables_of(near, far, model_blocks):
     count = near.shape[0]
     at = lax.iota(jnp.int32, count)
-    earlier = (near[:, None] == near[None, :]) & (at[:, None] < at[None, :])
-    spot = near * COL_TILES + jnp.sum(earlier.astype(jnp.int32), axis=0)
+    before = at[:, None] < at[None, :]
+    equal = far[:, None] == far[None, :]
+    spot = near * COL_TILES + jnp.sum(((near[:, None] == near[None, :]) & before).astype(jnp.int32), axis=0)
     here = spot[:, None] == at[None, :]
-    order = jnp.sum(jnp.where(here, at[:, None], 0), axis=0)
-    far_order = jnp.sum(jnp.where(here, far[:, None], 0), axis=0)
-    return order, far_order
+    packed = jnp.sum(jnp.where(here, (at * model_blocks + far)[:, None], 0), axis=0)
+    rank = jnp.sum((equal & before).astype(jnp.int32), axis=0)
+    place_of = rank + jnp.sum((far[:, None] < far[None, :]).astype(jnp.int32), axis=0)
+    there = place_of[:, None] == at[None, :]
+    code = (at * count + near) * 2 + (rank == 0)
+    far_packed = jnp.sum(jnp.where(there, code[:, None], 0), axis=0)
+    block = lax.iota(jnp.int32, model_blocks)
+    matches = far[:, None] == block[None, :]
+    until = jnp.sum((far[:, None] <= block[None, :]).astype(jnp.int32), axis=0)
+    last = jnp.where(jnp.any(matches, axis=0), until - 1, -1)
+    far_code = far_packed // 2
+    return (
+        packed // model_blocks, packed % model_blocks,
+        far_code // count, far_code % count, far_packed % 2, last,
+    )
 
 
 def body(sizes, activations, cotangent, up_tiles, down_tiles, up_rows, up_cols, down_rows, down_cols):
-    up_order, up_far = tables_of(up_cols[:, 0], up_rows[:, 0])
-    down_order, down_far = tables_of(down_rows[:, 0], down_cols[:, 0])
-    full = gather(sizes, activations, cotangent, up_tiles, down_tiles)
-    parts = local((up_order, up_far, down_order, down_far), *full)
-    out, inp, ga_u, ga_d, gb_u, gb_d = reduce(sizes, *parts)
+    ur, uc, dr, dc = (v[:, 0] for v in (up_rows, up_cols, down_rows, down_cols))
+    model_blocks = sizes[0] * activations.shape[1] // 128
+    sort = jax.vmap(functools.partial(tables_of, model_blocks=model_blocks))
+    order, far, far_order, far_near, far_first, last = sort(jnp.stack([uc, dr]), jnp.stack([ur, dc]))
+    x, cot, up, down = gather(sizes, activations, cotangent, up_tiles, down_tiles)
+    hidden, slope, xt = forward(order[0], far[0], x, up)
+    tables = (
+        order[1], far[1], ur, uc, dr, dc,
+        far_order[0], far_near[0], far_first[0], last[0],
+        far_order[1], far_near[1], far_first[1], last[1],
+    )
+    out, inp, ga_u, ga_d, gb_u, gb_d = reduce(sizes, tables, hidden, slope, xt, cot, up, down)
 
     def flat(v):
         return v.transpose(1, 0, 2).reshape(v.shape[1], -1)

time: 255 us -> 240 us (0.941)
  Pallas kernels: 237 us -> 222 us
  local copies, waits for them, and re-layouts: 3.78 us -> 7.19 us
    pallas_call x1, Pallas kernels: 50.6 us -> 18.6 us  [forward(): pl.pallas_call(functools.partial(forward_kernel, hidden_blocks), out_shap...]
    pallas_call x1, Pallas kernels: 109 us -> 127 us  [reduce(): pl.pallas_call(functools.partial(reduce_kernel, sizes), out_shape=[jax.Sh...]
    slice x0 -> x5, local copies, waits for them, and re-layouts: none -> 2.92 us  [the longest x2 1.17 us: body(): hidden, slope, xt = forward(order[0], far[0], x, up)]
where the time goes in v3:
time: 240 us
  Pallas kernels  222 us (92%)
  other arithmetic  9.8 us (4%)
  local copies, waits for them, and re-layouts  7.19 us (3%)
    pallas_call x1, Pallas kernels, reduce(): pl.pallas_call(functools.partial(reduce_kernel, sizes), out_shape=[jax.Sh...  127 us
    pallas_call x1, Pallas kernels, gather(): pl.pallas_call(functools.partial(gather_kernel, sizes), out_shape=(jax.Sh...  76.9 us
    pallas_call x1, Pallas kernels, forward(): pl.pallas_call(functools.partial(forward_kernel, hidden_blocks), out_shap...  18.6 us
    add x2, other arithmetic, total(): return a.astype(jnp.float32) + jnp.sum(b.astype(jnp.float32), axis=0)  7.33 us

profile of v3, /device:TPU:8, one launch (start us, length us, event | category | flops | bytes accessed | tf_op | source)
XLA Modules:
  0.0 240.1 jit_solution(8046195381062026911)
XLA Ops:
  0.7 0.7 pad_add_fusion.1
  1.4 0.1 fusion
  1.5 0.1 convert_reduce_fusion.3
  1.6 0.5 slice_bitcast_fusion
  2.2 0.3 convert_reduce_fusion.1
  2.4 0.7 fusion.7
  3.2 0.2 select_reduce_fusion.1
  3.4 0.2 select_reduce_fusion
  3.6 0.6 fusion.2
  4.2 0.6 fusion.3
  4.8 0.6 fusion.5
  5.4 0.6 fusion.6
  6.0 0.6 fusion.4
  6.6 76.9 %gather_all.1 = (bf16[64,128,128]{2,1,0:T(8,128)(2,1)}, bf16[64,128,128]{2,1,0:T(8,128)(2,1)}, bf16[256,128,128]{2,1,0:T(8,128)(2,1)}, bf16[256,128,128]{2,1,0:T(8,128)(2,1)}) custom-call(bf16[128,2048]{1,0:T(8,128)(2,1)} %act.1, bf16[128,2048]{1,0:T(8,128)(2,1)} %cot.1, bf16[64,128,128]{2,1,0:T(8,128)(2,1)} %up.1, bf16[64,128,128]{2,1,0:T(8,128)(2,1)} %down.1), custom_call_target="tpu_custom_call" | custom-call | tf_op jit(solution)/shard_map/gather_all/pallas_call | solution.py:233
  83.5 18.6 %forward_work.1 = (bf16[32,128,128]{2,1,0:T(8,128)(2,1)}, f32[32,128,128]{2,1,0:T(8,128)}, bf16[64,128,128]{2,1,0:T(8,128)(2,1)}) custom-call(s32[256]{0:T(256)} %bitcast.47, s32[256]{0:T(256)} %bitcast.44, bf16[64,128,128]{2,1,0:T(8,128)(2,1)} %get-tuple-element.17.x, bf16[256,128,128]{2,1,0:T(8,128)(2,1)} %get-tuple-element.18.u.up), custom_call_target="tpu_custom_call" | custom-call | tf_op jit(solution)/shard_map/forward_work/pallas_call | solution.py:289
  102.1 126.9 %reduce_all.1 = (bf16[16,128,128]{2,1,0:T(8,128)(2,1)}, bf16[16,128,128]{2,1,0:T(8,128)(2,1)}, bf16[64,128,128]{2,1,0:T(8,128)(2,1)}, bf16[64,128,128]{2,1,0:T(8...) custom-call(s32[256]{0:T(256)} %bitcast.43, s32[256]{0:T(256)} %bitcast.42, ...), custom_call_target="tpu_custom_call" | custom-call | tf_op jit(solution)/shard_map/reduce_all/pallas_call | solution.py:599
  229.0 0.0 copy-start.3
  229.0 0.0 copy-start.2
  229.0 1.5 copy.16
  230.5 1.0 copy.18
  231.5 0.0 copy-done.3
  231.5 0.3 copy.17
  231.8 1.0 copy.19
  232.8 0.0 copy-done.2
  232.8 0.0 copy-start
  232.8 0.0 copy-start.1
  232.8 4.5 %convert_add_fusion.1 = f32[64,128,128]{2,1,0:T(8,128)} fusion(bf16[64,128,128]{2,1,0:T(8,128)(2,1)S(1)} %copy-done.2, bf16[1,64,128,128]{3,2,1,0:T(8,128)(2,1)} %get-tuple-element.27), kind=kLoop, calls=%fused_computation.1 | loop fusion | flops 3145728 | bytes 8388608 | tf_op jit(solution)/shard_map/add | solution.py:682
  237.3 0.0 copy-done
  237.3 0.0 copy-done.1
  237.3 2.8 %convert_add_fusion = f32[64,128,128]{2,1,0:T(8,128)} fusion(bf16[64,128,128]{2,1,0:T(8,128)(2,1)S(1)} %copy-done, bf16[1,64,128,128]{3,2,1,0:T(8,128)(2,1)S(1)} %copy-done.1), kind=kLoop, calls=%fused_computation | loop fusion | flops 3145728 | bytes 8388608 | tf_op jit(solution)/shard_map/add | solution.py:682
  (7 shorter events, 0.1 us)
Async XLA Ops:
  229.0 2.5 %copy-start.3 = (bf16[16,128,128]{2,1,0:T(8,128)(2,1)S(1)}, bf16[16,128,128]{2,1,0:T(8,128)(2,1)}, u32[]{:S(2)}) copy-start(bf16[16,128,128]{2,1,0:T(8,128)(2,1)} %get-tuple-element.25) | copy-start | bytes 1572868
  229.0 3.8 %copy-start.2 = (bf16[64,128,128]{2,1,0:T(8,128)(2,1)S(1)}, bf16[64,128,128]{2,1,0:T(8,128)(2,1)}, u32[]{:S(2)}) copy-start(bf16[64,128,128]{2,1,0:T(8,128)(2,1)} %get-tuple-element.26) | copy-start | bytes 6291460
  232.8 4.5 %copy-start = (bf16[64,128,128]{2,1,0:T(8,128)(2,1)S(1)}, bf16[64,128,128]{2,1,0:T(8,128)(2,1)}, u32[]{:S(2)}) copy-start(bf16[64,128,128]{2,1,0:T(8,128)(2,1)} %get-tuple-element.28) | copy-start | bytes 6291460
  232.8 4.5 %copy-start.1 = (bf16[1,64,128,128]{3,2,1,0:T(8,128)(2,1)S(1)}, bf16[1,64,128,128]{3,2,1,0:T(8,128)(2,1)}, u32[]{:S(2)}) copy-start(bf16[1,64,128,128]{3,2,1,0:T(8,128)(2,1)} %get-tuple-element.29) | copy-start | bytes 6291460

commit v4 on v3

--- a/solution.py
+++ b/solution.py
@@ -1,5 +1,4 @@
 import functools
-from itertools import zip_longest
 
 import jax
 import jax.numpy as jnp
@@ -63,16 +62,17 @@
 
 
 def gather_kernel(
-    sizes, act, cot, up, down, x_all, c_all, u_all, d_all,
-    own_x, own_c, own_u, own_d,
+    sizes, uo, uf, act, cot, up, down, c_all, u_all, d_all, hidden, slope, xt,
+    x_all, u_held, own_c, own_u, own_d,
     load_sem, keep_sem, zs_sem, zr_sem, xs_sem, xr_sem, ys_sem, yr_sem, cs_sem, cr_sem,
 ):
     n, chips, replicas = sizes
     z, r, c, y = place(sizes)
     f = r * 2 + c
-    blocks = own_x.shape[0]
+    blocks = own_c.shape[0]
     per = up.shape[0]
     part = per // replicas
+    own_x = x_all.at[pl.ds(z * blocks, blocks)]
     features = ((act, own_x, x_all), (cot, own_c, c_all))
     weights = ((up, own_u, u_all), (down, own_d, d_all))
 
@@ -109,13 +109,15 @@
     def has(s, way):
         return z - s >= 0 if way > 0 else z + s <= n - 1
 
-    for a in range(2):
+    def z_start(a):
         for way in (1, -1):
 
             @pl.when(can_send(way))
             def _():
                 line(a, 0, way, True).start()
 
+    z_start(0)
+
     def tile_range(full, r_of, c_of, q):
         return full.at[pl.ds((r_of * 2 + c_of) * per + q * part, part)]
 
@@ -141,12 +143,11 @@
         own_core(a).start()
 
     keeps = []
-    for a, (_, own, full) in enumerate(features):
-        keeps.append(pltpu.make_async_copy(own, shard(full, z), keep_sem.at[a]))
+    keeps.append(pltpu.make_async_copy(own_c, shard(c_all, z), keep_sem.at[0]))
     for a, (src, own, full) in enumerate(weights):
         pltpu.make_async_copy(src, own, load_sem.at[2 + a, 0]).wait()
         keeps.append(
-            pltpu.make_async_copy(own, full.at[pl.ds(f * per, per)], keep_sem.at[2 + a])
+            pltpu.make_async_copy(own, full.at[pl.ds(f * per, per)], keep_sem.at[1 + a])
         )
     for copy in keeps:
         copy.start()
@@ -165,19 +166,18 @@
             piece, piece, cs_sem.at[a, d, e], cr_sem.at[a, d, e], {"fsdp": r * 2 + 1 - c}
         )
 
-    def z_event(s):
-        for a in range(2):
-            for way in (1, -1):
-
-                @pl.when(has(s, way))
-                def _():
-                    line(a, s - 1, way, False).wait_recv()
-
-                    if s < n - 1:
-
-                        @pl.when(can_send(way))
-                        def _():
-                            line(a, s, way, False).start()
+    def z_event(a, s):
+        for way in (1, -1):
+
+            @pl.when(has(s, way))
+            def _():
+                line(a, s - 1, way, False).wait_recv()
+
+                if s < n - 1:
+
+                    @pl.when(can_send(way))
+                    def _():
+                        line(a, s, way, False).start()
 
     def x_event(a):
         for d in range(1, chips):
@@ -192,28 +192,70 @@
                 y_copy(a, d, e).wait_recv()
                 core_copy(a, d, e).start()
 
-    tile_events = [
-        lambda: x_event(0),
-        lambda: (x_event(1), y_event(0)),
-        lambda: y_event(1),
-    ]
-    z_events = [functools.partial(z_event, s) for s in range(1, n)]
-    for first, second in zip_longest(z_events, tile_events):
-        if first is not None:
-            first()
-        if second is not None:
-            second()
-
-    for copy in keeps:
-        copy.wait()
+    load_up = pltpu.make_async_copy(u_all, u_held, load_sem.at[4, 0])
+
+    def fetch_up():
+        keeps[1].wait()
+        own_core(0).wait_recv()
+        for d in range(1, chips):
+            for e in range(replicas):
+                core_copy(0, d, e).wait_recv()
+        load_up.start()
+        load_up.wait()
+
+    def turn():
+        @pl.loop(0, x_all.shape[0])
+        def _(b):
+            xt[b] = x_all[b].T
+
+    hidden_blocks = hidden.shape[0]
+
+    def forward_part(g):
+        span = hidden_blocks // 4
+
+        @pl.loop(g * span, (g + 1) * span)
+        def _(h):
+            first = h * COL_TILES
+            pre = mm(x_all[uf[first]], u_held[uo[first]], 1, 0)
+            for k in range(1, COL_TILES):
+                pre += mm(x_all[uf[first + k]], u_held[uo[first + k]], 1, 0)
+            value, tangent = gelu_parts(pre)
+            hidden[h] = value.astype(jnp.bfloat16)
+            slope[h] = tangent
+
+    for s in range(1, n - 1):
+        z_event(0, s)
+    z_start(1)
+    x_event(0)
+    z_event(0, n - 1)
+    turn()
+    x_event(1)
+    y_event(0)
+    later = [functools.partial(z_event, 1, s) for s in range(1, n - 1)]
+    later.pop(0)()
+    fetch_up()
+    forward_part(0)
+    forward_part(1)
+    for event in later:
+        event()
+    forward_part(2)
+    y_event(1)
+    forward_part(3)
+    z_event(1, n - 1)
+
+    keeps[0].wait()
+    keeps[2].wait()
+    own_core(1).wait_recv()
     for a in range(2):
-        own_core(a).wait()
+        own_core(a).wait_send()
         for d in range(1, chips):
             x_copy(a, d).wait_send()
-            core_copy(a, d, 0).wait()
+            for e in range(replicas):
+                core_copy(a, d, e).wait_send()
+                if a == 1:
+                    core_copy(a, d, e).wait_recv()
             for e in range(1, replicas):
                 y_copy(a, d, e).wait_send()
-                core_copy(a, d, e).wait()
         for way in (1, -1):
             for s in range(n - 1):
 
@@ -222,31 +264,37 @@
                     line(a, s, way, s == 0).wait_send()
 
 
-def gather(sizes, activations, cotangent, up_tiles, down_tiles):
+def gather(sizes, order, far, activations, cotangent, up_tiles, down_tiles):
     n, chips, replicas = sizes
     rows, wide = activations.shape
     blocks = wide // 128
     per = up_tiles.shape[0]
+    hidden_blocks = 2 * chips * per // COL_TILES
     kind = jnp.bfloat16
     dma = pltpu.SemaphoreType.DMA
+    vmem = pl.BlockSpec(memory_space=pltpu.VMEM)
+    smem = pl.BlockSpec(memory_space=pltpu.SMEM)
     anywhere = pl.BlockSpec(memory_space=pl.ANY)
     return pl.pallas_call(
         functools.partial(gather_kernel, sizes),
         out_shape=(
             jax.ShapeDtypeStruct((n * blocks, rows, 128), kind),
-            jax.ShapeDtypeStruct((n * blocks, rows, 128), kind),
             jax.ShapeDtypeStruct((2 * chips * per, 128, 128), kind),
             jax.ShapeDtypeStruct((2 * chips * per, 128, 128), kind),
+            jax.ShapeDtypeStruct((hidden_blocks, rows, 128), kind),
+            jax.ShapeDtypeStruct((hidden_blocks, rows, 128), jnp.float32),
+            jax.ShapeDtypeStruct((n * blocks, 128, rows), kind),
         ),
-        in_specs=[anywhere] * 4,
-        out_specs=(anywhere,) * 4,
+        in_specs=[smem] * 2 + [anywhere] * 4,
+        out_specs=(anywhere,) * 3 + (vmem,) * 3,
         scratch_shapes=[
-            pltpu.VMEM((blocks, rows, 128), kind),
+            pltpu.VMEM((n * blocks, rows, 128), kind),
+            pltpu.VMEM((2 * chips * per, 128, 128), kind),
             pltpu.VMEM((blocks, rows, 128), kind),
             pltpu.VMEM((per, 128, 128), kind),
             pltpu.VMEM((per, 128, 128), kind),
-            dma((4, blocks)),
-            dma((4,)),
+            dma((5, blocks)),
+            dma((3,)),
             dma((2, 2, n)),
             dma((2, 2, n)),
             dma((2, chips)),
@@ -256,48 +304,15 @@
             dma((2, chips, replicas)),
             dma((2, chips, replicas)),
         ],
-        compiler_params=pltpu.CompilerParams(collective_id=0, has_side_effects=True),
+        compiler_params=pltpu.CompilerParams(
+            collective_id=0, has_side_effects=True, vmem_limit_bytes=60 * 1024 * 1024
+        ),
         name="gather_all",
-    )(activations, cotangent, up_tiles, down_tiles)
+    )(order, far, activations, cotangent, up_tiles, down_tiles)
 
 
 def mm(a, b, ca, cb):
     return lax.dot_general(a, b, (((ca,), (cb,)), ((), ())), preferred_element_type=jnp.float32)
-
-
-def forward_kernel(hidden_blocks, uo, uf, x, u, hidden, slope, xt):
-    @pl.loop(0, x.shape[0])
-    def _(b):
-        xt[b] = x[b].T
-
-    @pl.loop(0, hidden_blocks)
-    def _(h):
-        first = h * COL_TILES
-        pre = mm(x[uf[first]], u[uo[first]], 1, 0)
-        for k in range(1, COL_TILES):
-            pre += mm(x[uf[first + k]], u[uo[first + k]], 1, 0)
-        value, tangent = gelu_parts(pre)
-        hidden[h] = value.astype(jnp.bfloat16)
-        slope[h] = tangent
-
-
-def forward(order, far, x, u):
-    vmem = pl.BlockSpec(memory_space=pltpu.VMEM)
-    smem = pl.BlockSpec(memory_space=pltpu.SMEM)
-    hidden_blocks = u.shape[0] // COL_TILES
-    rows = x.shape[1]
-    return pl.pallas_call(
-        functools.partial(forward_kernel, hidden_blocks),
-        out_shape=(
-            jax.ShapeDtypeStruct((hidden_blocks, rows, 128), jnp.bfloat16),
-            jax.ShapeDtypeStruct((hidden_blocks, rows, 128), jnp.float32),
-            jax.ShapeDtypeStruct((x.shape[0], 128, rows), jnp.bfloat16),
-        ),
-        in_specs=[smem] * 2 + [vmem] * 2,
-        out_specs=(vmem,) * 3,
-        compiler_params=pltpu.CompilerParams(vmem_limit_bytes=60 * 1024 * 1024),
-        name="forward_work",
-    )(order, far, x, u)
 
 
 def add_into(target, terms):
@@ -508,8 +523,9 @@
 
     for k in range(PIECES):
         hand_over(0, k)
-    for k in range(PIECES):
-        feed(0, k)
+        if k >= 1:
+            feed(0, k - 1)
+    feed(0, PIECES - 1)
     load_d.wait()
     load_u.wait()
     work = (
@@ -527,21 +543,17 @@
         for step in work[:3]:
             step()
         work = work[3:]
-        if not work and handed < PIECES:
-            hand_over(1, handed)
-            handed += 1
-        if not work and handed >= 2 and fed < handed - 1:
-            feed(1, fed)
-            fed += 1
-        if i >= 5 and i % 2 == 1 and slots:
+        if not work:
+            for _ in range(2):
+                if handed < PIECES:
+                    hand_over(1, handed)
+                    handed += 1
+            for _ in range(2):
+                if fed < handed - 1 or fed < handed == PIECES:
+                    feed(1, fed)
+                    fed += 1
+        if i in (5, 7, 11, 13) and slots:
             z_event(*slots.pop(0))
-        if i == PIECES - 1:
-            while handed < PIECES:
-                hand_over(1, handed)
-                handed += 1
-        if i >= PIECES - 1 and fed < PIECES:
-            feed(1, fed)
-            fed += 1
         x_event(*piece)
     for slot in slots:
         z_event(*slot)
@@ -666,8 +678,9 @@
     model_blocks = sizes[0] * activations.shape[1] // 128
     sort = jax.vmap(functools.partial(tables_of, model_blocks=model_blocks))
     order, far, far_order, far_near, far_first, last = sort(jnp.stack([uc, dr]), jnp.stack([ur, dc]))
-    x, cot, up, down = gather(sizes, activations, cotangent, up_tiles, down_tiles)
-    hidden, slope, xt = forward(order[0], far[0], x, up)
+    cot, up, down, hidden, slope, xt = gather(
+        sizes, order[0], far[0], activations, cotangent, up_tiles, down_tiles
+    )
     tables = (
         order[1], far[1], ur, uc, dr, dc,
         far_order[0], far_near[0], far_first[0], last[0],

time: 240 us -> 225 us (0.938)
  Pallas kernels: 222 us -> 206 us
    pallas_call x1 -> x0, Pallas kernels: 18.6 us -> none  [forward(): pl.pallas_call(functools.partial(forward_kernel, hidden_blocks), out_shap...]
    pallas_call x1, Pallas kernels: 76.9 us -> 80.9 us  [gather(): pl.pallas_call(functools.partial(gather_kernel, sizes), out_shape=(jax.Sh...]
where the time goes in v4:
time: 225 us; the launch traced here: 223 us
  Pallas kernels  206 us (92%)
  other arithmetic  9.8 us (4%)
  local copies, waits for them, and re-layouts  7.16 us (3%)
    pallas_call x1, Pallas kernels, reduce(): pl.pallas_call(functools.partial(reduce_kernel, sizes), out_shape=[jax.Sh...  125 us
    pallas_call x1, Pallas kernels, gather(): pl.pallas_call(functools.partial(gather_kernel, sizes), out_shape=(jax.Sh...  80.9 us
    add x2, other arithmetic, total(): return a.astype(jnp.float32) + jnp.sum(b.astype(jnp.float32), axis=0)  7.33 us

profile of v4, /device:TPU:8, one launch (start us, length us, event | category | flops | bytes accessed | tf_op | source)
XLA Modules:
  0.0 223.5 jit_solution(273213726665781657)
XLA Ops:
  0.7 0.7 pad_add_fusion.1
  1.4 0.1 fusion
  1.5 0.1 convert_reduce_fusion.3
  1.6 0.5 slice_bitcast_fusion
  2.2 0.3 convert_reduce_fusion.1
  2.5 0.7 fusion.7
  3.2 0.2 select_reduce_fusion.1
  3.4 0.2 select_reduce_fusion
  3.6 0.6 fusion.2
  4.2 0.6 fusion.3
  4.8 0.6 fusion.5
  5.4 0.6 fusion.6
  6.0 0.5 fusion.4
  6.5 80.9 %gather_all.1 = (bf16[64,128,128]{2,1,0:T(8,128)(2,1)}, bf16[256,128,128]{2,1,0:T(8,128)(2,1)}, bf16[256,128,128]{2,1,0:T(8,128)(2,1)}, bf16[32,128,128]{2,1,0:T...) custom-call(s32[256]{0:T(256)} %bitcast.47, s32[256]{0:T(256)} %bitcast.44, bf16[128,2048]{1,0:T(8,128)(2,1)} %act.1, ...), custom_call_target="tpu_custom_call" | custom-call | tf_op jit(solution)/shard_map/gather_all/pallas_call | solution.py:278
  87.4 124.9 %reduce_all.1 = (bf16[16,128,128]{2,1,0:T(8,128)(2,1)}, bf16[16,128,128]{2,1,0:T(8,128)(2,1)}, bf16[64,128,128]{2,1,0:T(8,128)(2,1)}, bf16[64,128,128]{2,1,0:T(8...) custom-call(s32[256]{0:T(256)} %bitcast.43, s32[256]{0:T(256)} %bitcast.42, ...), custom_call_target="tpu_custom_call" | custom-call | tf_op jit(solution)/shard_map/reduce_all/pallas_call | solution.py:611
  212.3 0.0 copy-start.3
  212.3 0.0 copy-start.2
  212.3 1.5 copy.16
  213.8 1.0 copy.18
  214.8 0.0 copy-done.3
  214.8 0.3 copy.17
  215.1 1.0 copy.19
  216.1 0.0 copy-done.2
  216.1 0.0 copy-start
  216.1 0.0 copy-start.1
  216.1 4.5 %convert_add_fusion.1 = f32[64,128,128]{2,1,0:T(8,128)} fusion(bf16[64,128,128]{2,1,0:T(8,128)(2,1)S(1)} %copy-done.2, bf16[1,64,128,128]{3,2,1,0:T(8,128)(2,1)} %get-tuple-element.25), kind=kLoop, calls=%fused_computation.1 | loop fusion | flops 3145728 | bytes 8388608 | tf_op jit(solution)/shard_map/add | solution.py:695
  220.6 0.0 copy-done
  220.6 0.0 copy-done.1
  220.6 2.8 %convert_add_fusion = f32[64,128,128]{2,1,0:T(8,128)} fusion(bf16[64,128,128]{2,1,0:T(8,128)(2,1)S(1)} %copy-done, bf16[1,64,128,128]{3,2,1,0:T(8,128)(2,1)S(1)} %copy-done.1), kind=kLoop, calls=%fused_computation | loop fusion | flops 3145728 | bytes 8388608 | tf_op jit(solution)/shard_map/add | solution.py:695
  (7 shorter events, 0.1 us)
Async XLA Ops:
  212.3 2.5 %copy-start.3 = (bf16[16,128,128]{2,1,0:T(8,128)(2,1)S(1)}, bf16[16,128,128]{2,1,0:T(8,128)(2,1)}, u32[]{:S(2)}) copy-start(bf16[16,128,128]{2,1,0:T(8,128)(2,1)} %get-tuple-element.23) | copy-start | bytes 1572868
  212.3 3.8 %copy-start.2 = (bf16[64,128,128]{2,1,0:T(8,128)(2,1)S(1)}, bf16[64,128,128]{2,1,0:T(8,128)(2,1)}, u32[]{:S(2)}) copy-start(bf16[64,128,128]{2,1,0:T(8,128)(2,1)} %get-tuple-element.24) | copy-start | bytes 6291460
  216.1 4.5 %copy-start = (bf16[64,128,128]{2,1,0:T(8,128)(2,1)S(1)}, bf16[64,128,128]{2,1,0:T(8,128)(2,1)}, u32[]{:S(2)}) copy-start(bf16[64,128,128]{2,1,0:T(8,128)(2,1)} %get-tuple-element.26) | copy-start | bytes 6291460
  216.1 4.5 %copy-start.1 = (bf16[1,64,128,128]{3,2,1,0:T(8,128)(2,1)S(1)}, bf16[1,64,128,128]{3,2,1,0:T(8,128)(2,1)}, u32[]{:S(2)}) copy-start(bf16[1,64,128,128]{3,2,1,0:T(8,128)(2,1)} %get-tuple-element.27) | copy-start | bytes 6291460

commit v5 on v4

--- a/solution.py
+++ b/solution.py
@@ -540,9 +540,9 @@
     handed = 0
     fed = 0
     for i, piece in enumerate(pieces):
-        for step in work[:3]:
+        for step in work[:5]:
             step()
-        work = work[3:]
+        work = work[5:]
         if not work:
             for _ in range(2):
                 if handed < PIECES:
@@ -552,7 +552,7 @@
                 if fed < handed - 1 or fed < handed == PIECES:
                     feed(1, fed)
                     fed += 1
-        if i in (5, 7, 11, 13) and slots:
+        if i in (4, 6, 10, 12) and slots:
             z_event(*slots.pop(0))
         x_event(*piece)
     for slot in slots:

time: 225 us -> 236 us (1.049)
  Pallas kernels: 206 us -> 216 us
    pallas_call x1, Pallas kernels: 125 us -> 135 us  [reduce(): pl.pallas_call(functools.partial(reduce_kernel, sizes), out_shape=[jax.Sh...]
where the time goes in v5:
time: 236 us; the launch traced here: 234 us
  Pallas kernels  216 us (92%)
  other arithmetic  9.8 us (4%)
  local copies, waits for them, and re-layouts  7.16 us (3%)
    pallas_call x1, Pallas kernels, reduce(): pl.pallas_call(functools.partial(reduce_kernel, sizes), out_shape=[jax.Sh...  135 us
    pallas_call x1, Pallas kernels, gather(): pl.pallas_call(functools.partial(gather_kernel, sizes), out_shape=(jax.Sh...  80.9 us
    add x2, other arithmetic, total(): return a.astype(jnp.float32) + jnp.sum(b.astype(jnp.float32), axis=0)  7.33 us

profile of v5, /device:TPU:8, one launch (start us, length us, event | category | flops | bytes accessed | tf_op | source)
XLA Modules:
  0.0 234.0 jit_solution(5495219786382385260)
XLA Ops:
  0.7 0.7 pad_add_fusion.1
  1.4 0.1 fusion
  1.5 0.1 convert_reduce_fusion.3
  1.6 0.5 slice_bitcast_fusion
  2.2 0.3 convert_reduce_fusion.1
  2.5 0.7 fusion.7
  3.2 0.2 select_reduce_fusion.1
  3.4 0.2 select_reduce_fusion
  3.6 0.6 fusion.2
  4.2 0.6 fusion.3
  4.8 0.6 fusion.5
  5.4 0.6 fusion.6
  6.0 0.5 fusion.4
  6.5 80.9 %gather_all.1 = (bf16[64,128,128]{2,1,0:T(8,128)(2,1)}, bf16[256,128,128]{2,1,0:T(8,128)(2,1)}, bf16[256,128,128]{2,1,0:T(8,128)(2,1)}, bf16[32,128,128]{2,1,0:T...) custom-call(s32[256]{0:T(256)} %bitcast.47, s32[256]{0:T(256)} %bitcast.44, bf16[128,2048]{1,0:T(8,128)(2,1)} %act.1, ...), custom_call_target="tpu_custom_call" | custom-call | tf_op jit(solution)/shard_map/gather_all/pallas_call | solution.py:278
  87.4 135.4 %reduce_all.1 = (bf16[16,128,128]{2,1,0:T(8,128)(2,1)}, bf16[16,128,128]{2,1,0:T(8,128)(2,1)}, bf16[64,128,128]{2,1,0:T(8,128)(2,1)}, bf16[64,128,128]{2,1,0:T(8...) custom-call(s32[256]{0:T(256)} %bitcast.43, s32[256]{0:T(256)} %bitcast.42, ...), custom_call_target="tpu_custom_call" | custom-call | tf_op jit(solution)/shard_map/reduce_all/pallas_call | solution.py:611
  222.8 0.0 copy-start.3
  222.9 0.0 copy-start.2
  222.9 1.5 copy.16
  224.3 1.0 copy.18
  225.3 0.0 copy-done.3
  225.3 0.3 copy.17
  225.6 1.0 copy.19
  226.6 0.0 copy-done.2
  226.6 0.0 copy-start
  226.6 0.0 copy-start.1
  226.7 4.5 %convert_add_fusion.1 = f32[64,128,128]{2,1,0:T(8,128)} fusion(bf16[64,128,128]{2,1,0:T(8,128)(2,1)S(1)} %copy-done.2, bf16[1,64,128,128]{3,2,1,0:T(8,128)(2,1)} %get-tuple-element.25), kind=kLoop, calls=%fused_computation.1 | loop fusion | flops 3145728 | bytes 8388608 | tf_op jit(solution)/shard_map/add | solution.py:695
  231.2 0.0 copy-done
  231.2 0.0 copy-done.1
  231.2 2.8 %convert_add_fusion = f32[64,128,128]{2,1,0:T(8,128)} fusion(bf16[64,128,128]{2,1,0:T(8,128)(2,1)S(1)} %copy-done, bf16[1,64,128,128]{3,2,1,0:T(8,128)(2,1)S(1)} %copy-done.1), kind=kLoop, calls=%fused_computation | loop fusion | flops 3145728 | bytes 8388608 | tf_op jit(solution)/shard_map/add | solution.py:695
  (7 shorter events, 0.1 us)
Async XLA Ops:
  222.8 2.5 %copy-start.3 = (bf16[16,128,128]{2,1,0:T(8,128)(2,1)S(1)}, bf16[16,128,128]{2,1,0:T(8,128)(2,1)}, u32[]{:S(2)}) copy-start(bf16[16,128,128]{2,1,0:T(8,128)(2,1)} %get-tuple-element.23) | copy-start | bytes 1572868
  222.9 3.8 %copy-start.2 = (bf16[64,128,128]{2,1,0:T(8,128)(2,1)S(1)}, bf16[64,128,128]{2,1,0:T(8,128)(2,1)}, u32[]{:S(2)}) copy-start(bf16[64,128,128]{2,1,0:T(8,128)(2,1)} %get-tuple-element.24) | copy-start | bytes 6291460
  226.6 4.5 %copy-start = (bf16[64,128,128]{2,1,0:T(8,128)(2,1)S(1)}, bf16[64,128,128]{2,1,0:T(8,128)(2,1)}, u32[]{:S(2)}) copy-start(bf16[64,128,128]{2,1,0:T(8,128)(2,1)} %get-tuple-element.26) | copy-start | bytes 6291460
  226.6 4.5 %copy-start.1 = (bf16[1,64,128,128]{3,2,1,0:T(8,128)(2,1)S(1)}, bf16[1,64,128,128]{3,2,1,0:T(8,128)(2,1)}, u32[]{:S(2)}) copy-start(bf16[1,64,128,128]{3,2,1,0:T(8,128)(2,1)} %get-tuple-element.27) | copy-start | bytes 6291460
